TPU v7x, 32 devices: a whole 2x2x4 slice. The times are simulated.
32 devices in a mesh: layer: 4 (over y, core), lat: 8 (over z, x).
Axes of the slice: x: 2, y: 2, z: 4, core: 2. Of those that a mesh axis runs over, the one named last changes fastest.
Arguments:
- residuals: bfloat16 [4, 256, 2048], P(None, ('layer', 'lat')), may hold values from -1100 to 1100
- topk_slots: int32 [4, 256, 64], P(None, ('layer', 'lat')), may hold values from -1 to 32767, as said below
- dictionary: bfloat16 [4, 32768, 2048], P('layer', 'lat'), may hold values from -80 to 80
- enc_bias: float32 [4, 32768], P('layer', 'lat'), may hold values from 0.5 to 3
- dec_bias: float32 [4, 2048], P('layer'), may hold values from -5 to 5
- dead_ids: int32 [4, 128], P('layer'), may hold values from 0 to 32767, as said below
- seed_tokens: int32 [4, 128], P('layer'), may hold values from 0 to 255
Outputs:
- reconstruction: bfloat16 [4, 256, 2048], P(None, ('layer', 'lat'))
- unexplained: float32 [4], P('layer')
- latent_mass: float32 [4, 32768], P('layer', 'lat')
- new_rows: bfloat16 [4, 128, 2048], P('layer', 'lat')
- new_bias: float32 [4, 32768], P('layer', 'lat')
Inputs may be any that keep to these rules, and one draw needn't show every extreme that they name: `topk_slots`: slot s of a token belongs to latent shard s // 8: it holds -1 or an id from (s // 8) * 4096 to (s // 8 + 1) * 4096 - 1. Every token has exactly 32 slots that are not -1; ids may repeat. In every layer some token fills all 8 slots of one shard. `dead_ids`: the 128 ids of one layer are distinct.
All inputs are finite; a program needn't handle non-finite values.
Results may differ from a plain program's by a relative error of at most 0.009.
Values may be sent and summed in bfloat16 or wider, within the bound.
No kernel may reach another device: no remote copies, remote signals or barrier semaphores. Data moves between devices by JAX's collectives and lax.ppermute only.
A program may use at most 128 MiB of HBM per device.

v0:
```python
import jax
import jax.numpy as jnp
from jax import lax
from jax.sharding import PartitionSpec as P


def token_position(global_tokens, tok_dev, lat_count, tok_group):
    blocks = global_tokens // tok_dev
    return blocks % lat_count * tok_group + blocks // lat_count * tok_dev + global_tokens % tok_dev


def body(residuals, topk_slots, dictionary, enc_bias, dec_bias, dead_ids, seed_tokens):
    layer_count = residuals.shape[0]
    tok_dev = residuals.shape[1]
    feature_width = residuals.shape[2]
    lat_count = lax.axis_size("lat")
    layer_size = lax.axis_size("layer")
    shard_index = lax.axis_index("lat")
    group_index = lax.axis_index("layer")
    lat_dev = dictionary.shape[1]
    tok_group = tok_dev * layer_size
    shard_rows = dictionary[0]
    row_norms = jnp.sqrt(jnp.sum(jnp.square(shard_rows.astype(jnp.float32)), axis=1) + 1e-06)
    norm_part = jnp.sum(row_norms)
    layer_slots = jnp.arange(layer_count, dtype=jnp.int32)
    norm_vector = jnp.where(layer_slots == group_index, norm_part, 0.0)
    squares = jnp.sum(jnp.square(residuals.astype(jnp.float32)), axis=(1, 2))
    totals, norm_totals = lax.psum((squares, norm_vector), ("layer", "lat"))
    norm_sum = lax.dynamic_index_in_dim(norm_totals, group_index, 0, keepdims=False)
    scales = lax.rsqrt(totals / (tok_dev * layer_size * lat_count * feature_width))
    outgoing = (residuals.astype(jnp.float32) * scales[:, None, None]).astype(jnp.bfloat16)
    regrouped = lax.all_to_all(outgoing, "layer", split_axis=0, concat_axis=1, tiled=True)
    gathered = lax.all_gather(regrouped, "lat", axis=1, tiled=True)
    features = gathered[0]
    mine_slots = lax.all_to_all(
        lax.all_to_all(topk_slots, "layer", split_axis=0, concat_axis=1, tiled=True),
        "lat",
        split_axis=2,
        concat_axis=1,
        tiled=True,
    )
    slot_major = mine_slots[0].T
    shifts = jnp.dot(
        shard_rows, dec_bias[0], precision=lax.Precision.HIGHEST, preferred_element_type=jnp.float32
    )
    is_live = slot_major >= 0
    clipped = jnp.where(is_live, slot_major - shard_index * lat_dev, 0)
    picked = jnp.take(shard_rows, clipped, axis=0)
    products = jnp.einsum("td,ctd->ct", features, picked, preferred_element_type=jnp.float32)
    picked_norms = row_norms[clipped]
    preact = (products - shifts[clipped]) / picked_norms + enc_bias[0][clipped]
    activity = jnp.where(is_live, jnp.maximum(preact, 0.0), 0.0)
    coefficient = (activity / picked_norms).astype(jnp.bfloat16)
    partial_value = jnp.einsum(
        "ct,ctd->td", coefficient, picked, preferred_element_type=jnp.float32
    )
    latent_mass = (
        jnp.zeros((lat_dev,), jnp.float32).at[clipped.reshape(-1)].add(activity.reshape(-1))
    )
    r_dev = seed_tokens.shape[1] // lat_count
    summed = lax.psum(partial_value.astype(jnp.bfloat16), "lat").astype(jnp.float32)
    estimate = summed + dec_bias[0]
    errors = features.astype(jnp.float32) - estimate
    numerator = jnp.sum(jnp.square(errors))
    estimate_own = lax.dynamic_slice_in_dim(estimate, shard_index * tok_group, tok_group, 0)
    my_seeds = lax.dynamic_slice_in_dim(seed_tokens[0], shard_index * r_dev, r_dev, 0)
    seeds = jnp.take(errors, token_position(my_seeds, tok_dev, lat_count, tok_group), axis=0)
    feat32 = features.astype(jnp.float32)
    centered = feat32 - jnp.mean(feat32, axis=0)
    denominator = jnp.sum(jnp.square(centered))
    unexplained = (numerator / denominator).reshape(1)
    seed_norm = jnp.sqrt(jnp.sum(jnp.square(seeds), axis=1, keepdims=True) + 1e-06)
    new_rows = (seeds / seed_norm * (norm_sum / (lat_dev * lat_count))).astype(jnp.bfloat16)[None]
    candidates = shard_index * lat_dev + jnp.arange(lat_dev, dtype=jnp.int32)
    is_dead = jnp.any(dead_ids[0][:, None] == candidates[None, :], axis=0)
    new_bias = jnp.where(is_dead, 0.0, enc_bias[0])[None]
    reconstruction = lax.all_to_all(
        estimate_own.astype(jnp.bfloat16)[None], "layer", split_axis=1, concat_axis=0, tiled=True
    )
    return (reconstruction, unexplained, latent_mass[None], new_rows, new_bias)


def solution(mesh):
    in_specs = (
        P(None, ("layer", "lat"), None),
        P(None, ("layer", "lat"), None),
        P("layer", "lat", None),
        P("layer", "lat"),
        P("layer", None),
        P("layer", None),
        P("layer", None),
    )
    out_specs = (
        P(None, ("layer", "lat"), None),
        P("layer"),
        P("layer", "lat"),
        P("layer", "lat", None),
        P("layer", "lat"),
    )
    return jax.shard_map(body, mesh=mesh, in_specs=in_specs, out_specs=out_specs, check_vma=False)
```

profile of v0, /device:TPU:0, one launch (start us, length us, event | category | flops | bytes accessed | tf_op | source)
XLA Modules:
  0.0 291.3 jit_solution(2012086604669841985)
XLA Ops:
  7.2 1.4 reshape.393
  8.6 4.3 %all-to-all-start = ((s32[4,1,512]{2,1,0:T(1,128)}), s32[4,1,512]{2,1,0:T(1,128)S(1)}, u32[]{:S(2)}, u32[]{:S(2)}) async-start(s32[4,1,512]{2,1,0:T(1,128)} %reshape.393), calls=%async_computation | async-start | bytes 16384 | tf_op jit(solution)/shard_map/all_to_all | solution.py:36
  12.8 8.8 %multiply_reduce_fusion = f32[4096]{0:T(1024)S(1)} fusion(bf16[1,4096,2048]{2,1,0:T(8,128)(2,1)} %param.9), kind=kLoop, calls=%fused_computation.6 | loop fusion | flops 25161728 | bytes 16793600 | tf_op jit(solution)/shard_map/reduce_sum | solution.py:23
  21.6 0.6 fusion.32
  22.2 1.3 fusion.7
  23.5 0.0 copy-start.6
  23.6 0.0 copy-start
  23.6 0.0 copy-start.3
  23.6 0.0 copy-start.7
  23.6 13.0 %fusion.17 = f32[1,4096]{1,0:T(1,128)S(1)} fusion(f32[1,2048]{1,0:T(1,128)S(1)} %copy-done.5, bf16[1,4096,2048]{2,1,0:T(8,128)(2,1)S(1)} %copy-done.1), kind=kOutput, calls=%fused_computation.46 | convolution fusion | flops 100663296 | bytes 16801792 | tf_op jit(solution)/shard_map/dot_general | solution.py:43
  36.6 0.7 compare_select_fusion.4
  37.3 41.5 %all-reduce = (f32[4]{0:T(128)S(1)}, f32[4]{0:T(128)S(1)}) all-reduce(f32[4]{0:T(128)S(1)} %fusion.7, f32[4]{0:T(128)S(1)} %compare_select_fusion.4), channel_id=1, replica_groups=mesh['layer'=4,'lat'=8] {'layer','lat'}, use_global_device_ids=true, to_apply=%region_1.0 | all-reduce | flops 8 | bytes 64 | tf_op jit(solution)/shard_map/psum | solution.py:28
  78.8 0.3 compare_reduce_fusion
  79.1 0.6 reshape_select_fusion
  79.8 0.0 all-to-all-done
  79.8 0.5 broadcast.399
  80.3 0.7 reduce
  81.0 0.1 reshape.394
  81.0 0.1 copy.31
  81.1 0.7 reduce.1
  81.9 0.7 reshape.395
  82.5 5.3 %all-to-all-start.1 = ((s32[8,1,256]{2,1,0:T(1,128)}), s32[8,1,256]{2,1,0:T(1,128)S(1)}, u32[]{:S(2)}, u32[]{:S(2)}) async-start(s32[8,1,256]{2,1,0:T(1,128)} %reshape.395), calls=%async_computation.1 | async-start | bytes 16384 | tf_op jit(solution)/shard_map/all_to_all | solution.py:35
  87.9 0.7 fusion.8
  88.6 0.6 dynamic_slice.18
  89.8 4.5 %all-to-all-done.1 = s32[8,1,256]{2,1,0:T(1,128)S(1)} async-done(((s32[8,1,256]{2,1,0:T(1,128)}), s32[8,1,256]{2,1,0:T(1,128)S(1)}, u32[]{:S(2)}, u32[]{:S(2)}) %all-to-all-start.1) | async-done | bytes 8224 | tf_op jit(solution)/shard_map/all_to_all | solution.py:35
  94.4 3.3 %all-to-all-start.2 = ((bf16[4,8,2048]{2,1,0:T(8,128)(2,1)}), bf16[4,8,2048]{2,1,0:T(8,128)(2,1)S(1)}, u32[]{:S(2)}, u32[]{:S(2)}) async-start(bf16[4,8,2048]{2,1,0:T(8,128)(2,1)} %fusion.8), calls=%async_computation.2 | async-start | bytes 262144 | tf_op jit(solution)/shard_map/all_to_all | solution.py:32
  97.7 0.0 all-gather.2.cloned.1.call-start
  97.8 0.1 fusion.30
  97.9 0.7 reduce.2
  98.5 0.1 reshape.396
  98.7 3.6 %all-to-all-done.2 = bf16[4,8,2048]{2,1,0:T(8,128)(2,1)S(1)} async-done(((bf16[4,8,2048]{2,1,0:T(8,128)(2,1)}), bf16[4,8,2048]{2,1,0:T(8,128)(2,1)S(1)}, u32[]{:S(2)}, u32[]{:S(2)}) %all-to-all-start.2) | async-done | bytes 131104 | tf_op jit(solution)/shard_map/all_to_all | solution.py:32
  102.3 0.7 copy-done.4
  102.9 0.0 all-gather.2.cloned.1.call-update
  103.0 0.2 all-reduce.3.cloned.1.call-start
  103.2 0.1 sub.47
  103.3 0.1 ge.32
  103.4 24.4 %gather_fusion = bf16[2048,2048]{1,0:T(8,128)(2,1)} fusion(bf16[4096,2048]{1,0:T(8,128)(2,1)} %bitcast.142, s32[2048]{0:T(1024)S(1)} %broadcast_clamp_fusion), kind=kCustom, calls=%fused_computation | custom fusion | bytes 16785408 | tf_op jit(solution)/shard_map/jit(_take)/gather | solution.py:48
  127.9 11.8 %gather_fusion.2 = f32[2048]{0:T(1024)S(1)} fusion(f32[4096]{0:T(1024)S(1)} %get-tuple-element.13, s32[2048]{0:T(1024)S(1)} %broadcast_clamp_fusion), kind=kCustom, calls=%fused_computation.2 | custom fusion | bytes 24576 | tf_op jit(solution)/shard_map/gather | solution.py:50
  139.7 11.8 %gather_fusion.1 = f32[2048]{0:T(1024)S(1)} fusion(f32[4096]{0:T(1024)S(1)} %bitcast.141, s32[2048]{0:T(1024)S(1)} %broadcast_clamp_fusion), kind=kCustom, calls=%fused_computation.1 | custom fusion | bytes 24576 | tf_op jit(solution)/shard_map/gather | solution.py:51
  151.5 11.8 %gather_fusion.3 = f32[2048]{0:T(1024)S(1)} fusion(f32[4096]{0:T(1024)S(1)} %bitcast.140, s32[2048]{0:T(1024)S(1)} %broadcast_clamp_fusion), kind=kCustom, calls=%fused_computation.3 | custom fusion | bytes 24576 | tf_op jit(solution)/shard_map/gather | solution.py:51
  163.3 7.4 %broadcast_select_fusion = bf16[8,256,2048]{2,1,0:T(8,128)(2,1)} fusion(bf16[8,256,2048]{2,1,0:T(8,128)(2,1)} %bitcast.143, pred[8,256]{1,0:T(8,128)(4,1)S(1)} %compare_and_fusion), kind=kLoop, calls=%fused_computation.7 | loop fusion | flops 4194304 | bytes 16779264 | tf_op jit(solution)/shard_map/jit(_take)/select_n | solution.py:48
  170.7 9.7 %fusion.2 = f32[256,1,8]{2,1,0:T(1,128)S(1)} fusion(bf16[8,256,2048]{2,1,0:T(8,128)(2,1)} %broadcast_select_fusion, bf16[256,2048,1]{1,0,2:T(8,128)(2,1)} %bitcast.144), kind=kOutput, calls=%fused_computation.10 | convolution fusion | flops 8388608 | bytes 9445376 | tf_op jit(solution)/shard_map/td,ctd->ct/dot_general | solution.py:49
  180.5 0.1 copy.39
  180.6 0.2 copy.40
  180.7 9.8 %fusion = bf16[256,1,2048]{2,1,0:T(2,128)(2,1)S(1)} fusion(bf16[8,256,1]{0,2,1:T(2,128)(2,1)S(1)} %copy.40, bf16[8,256,2048]{2,1,0:T(8,128)(2,1)} %broadcast_select_fusion), kind=kOutput, calls=%fused_computation.8 | convolution fusion | flops 8388608 | bytes 9441280 | tf_op jit(solution)/shard_map/ct,ctd->td/dot_general | solution.py:54
  190.6 1.6 copy.55
  192.2 0.0 all-reduce.3.cloned.1.call-update
  192.2 0.1 compare_and_fusion.1
  192.4 11.9 %scatter_custom_fusion = f32[4096]{0:T(1024)} fusion(s32[2048]{0:T(1024)S(1)} %bitcast.160, f32[2048]{0:T(1024)S(1)} %bitcast.161, f32[]{:T(128)} %constant.103.clone.1), kind=kCustom, calls=%fused_computation.49 | custom fusion | flops 2048 | bytes 16388 | tf_op jit(solution)/shard_map/scatter-add | solution.py:58
  204.3 0.2 convert_reduce_fusion
  204.5 62.3 %all-reduce.3.cloned.1.call-done = bf16[256,2048]{1,0:T(8,128)(2,1)} async-done(((bf16[256,2048]{1,0:T(8,128)(2,1)}), bf16[256,2048]{1,0:T(8,128)(2,1)}) %all-reduce.3.cloned.1.call-update) | async-done | bytes 1048592 | tf_op jit(solution)/shard_map/psum | solution.py:61
  266.8 2.5 multiply_reduce_fusion.1
  269.3 0.6 gather_fusion.4
  270.0 0.2 multiply_reduce_fusion.2
  270.2 1.4 convert_add_fusion
  271.6 0.2 copy.57
  271.9 0.5 broadcast.402
  272.4 1.4 reduce.3
  273.8 0.8 reshape.397
  274.6 3.3 %all-to-all-start.3 = ((bf16[4,2,8192]{2,1,0:T(2,128)(2,1)}), bf16[4,2,8192]{2,1,0:T(2,128)(2,1)S(1)}, u32[]{:S(2)}, u32[]{:S(2)}) async-start(bf16[4,2,8192]{2,1,0:T(2,128)(2,1)} %reshape.397), calls=%async_computation.3 | async-start | bytes 262144 | tf_op jit(solution)/shard_map/all_to_all | solution.py:77
  277.9 0.7 fusion.12
  279.9 2.5 all-to-all-done.3
  282.5 0.1 reshape.398
  282.6 0.7 copy.56
  (33 shorter events, 0.2 us)
Async XLA Ops:
  8.6 71.2 %all-to-all-start = ((s32[4,1,512]{2,1,0:T(1,128)}), s32[4,1,512]{2,1,0:T(1,128)S(1)}, u32[]{:S(2)}, u32[]{:S(2)}) async-start(s32[4,1,512]{2,1,0:T(1,128)} %reshape.393), calls=%async_computation | async-start | bytes 16384 | tf_op jit(solution)/shard_map/all_to_all | solution.py:36
  12.8 10.7 %copy-start.1 = (bf16[1,4096,2048]{2,1,0:T(8,128)(2,1)S(1)}, bf16[1,4096,2048]{2,1,0:T(8,128)(2,1)}, u32[]{:S(2)}) copy-start(bf16[1,4096,2048]{2,1,0:T(8,128)(2,1)} %param.9) | copy-start | bytes 50331652
  12.8 10.7 %copy-start.5 = (f32[1,2048]{1,0:T(1,128)S(1)}, f32[1,2048]{1,0:T(1,128)}, u32[]{:S(2)}) copy-start(f32[1,2048]{1,0:T(1,128)} %param.11) | copy-start | bytes 24580
  23.5 55.2 %copy-start.6 = (s32[1,128]{1,0:T(1,128)S(1)}, s32[1,128]{1,0:T(1,128)}, u32[]{:S(2)}) copy-start(s32[1,128]{1,0:T(1,128)} %param.12) | copy-start | bytes 1540
  23.6 55.6 %copy-start = (f32[1,4096]{1,0:T(1,128)S(1)}, f32[1,4096]{1,0:T(1,128)}, u32[]{:S(2)}) copy-start(f32[1,4096]{1,0:T(1,128)} %param.10) | copy-start | bytes 49156
  23.6 64.3 %copy-start.3 = (bf16[4,8,2048]{2,1,0:T(8,128)(2,1)S(1)}, bf16[4,8,2048]{2,1,0:T(8,128)(2,1)}, u32[]{:S(2)}) copy-start(bf16[4,8,2048]{2,1,0:T(8,128)(2,1)} %param.7) | copy-start | bytes 393220
  23.6 74.2 %copy-start.7 = (s32[1,128]{1,0:T(1,128)S(1)}, s32[1,128]{1,0:T(1,128)}, u32[]{:S(2)}) copy-start(s32[1,128]{1,0:T(1,128)} %param.13) | copy-start | bytes 1540
  82.5 11.8 %all-to-all-start.1 = ((s32[8,1,256]{2,1,0:T(1,128)}), s32[8,1,256]{2,1,0:T(1,128)S(1)}, u32[]{:S(2)}, u32[]{:S(2)}) async-start(s32[8,1,256]{2,1,0:T(1,128)} %reshape.395), calls=%async_computation.1 | async-start | bytes 16384 | tf_op jit(solution)/shard_map/all_to_all | solution.py:35
  94.4 7.9 %all-to-all-start.2 = ((bf16[4,8,2048]{2,1,0:T(8,128)(2,1)}), bf16[4,8,2048]{2,1,0:T(8,128)(2,1)S(1)}, u32[]{:S(2)}, u32[]{:S(2)}) async-start(bf16[4,8,2048]{2,1,0:T(8,128)(2,1)} %fusion.8), calls=%async_computation.2 | async-start | bytes 262144 | tf_op jit(solution)/shard_map/all_to_all | solution.py:32
  97.7 73.0 %all-gather.2.cloned.1.call-start = ((), (), s32[]{:S(2)}) async-start(), calls=%async_computation.4 | async-start | bytes 1179648 | tf_op jit(solution)/shard_map/all_gather | solution.py:33
  102.3 0.7 copy-start.4
  103.0 163.9 %all-reduce.3.cloned.1.call-start = ((), (), s32[]{:S(2)}) async-start(), calls=%async_computation.5 | async-start | bytes 2097152 | tf_op jit(solution)/shard_map/psum | solution.py:61
  180.5 23.9 %copy-start.2 = (bf16[1,256,2048]{2,1,0:T(8,128)(2,1)S(1)}, bf16[1,256,2048]{2,1,0:T(8,128)(2,1)}, u32[]{:S(2)}) copy-start(bf16[1,256,2048]{2,1,0:T(8,128)(2,1)} %all-gather.2.cloned.1.call-done) | copy-start | bytes 3145732
  274.6 7.9 %all-to-all-start.3 = ((bf16[4,2,8192]{2,1,0:T(2,128)(2,1)}), bf16[4,2,8192]{2,1,0:T(2,128)(2,1)S(1)}, u32[]{:S(2)}, u32[]{:S(2)}) async-start(bf16[4,2,8192]{2,1,0:T(2,128)(2,1)} %reshape.397), calls=%async_computation.3 | async-start | bytes 262144 | tf_op jit(solution)/shard_map/all_to_all | solution.py:77
Sparse Core Ops, SparseCore 0:
  103.1 36.6 all-gather.1
  192.4 74.4 all-reduce.2
where the time goes:
time: 292 us; the launch traced here: 291 us
  waiting for transfers between devices  73.1 us (25%)
  local copies, waits for them, and re-layouts  69 us (24%)
  blocking collectives  41.5 us (14%)
  other arithmetic  41.2 us (14%)
  matrix products  32.6 us (11%)
  between operations  17.4 us (6%)
  starting transfers between devices  16.5 us (6%)
    psum x1, waiting for transfers between devices, body(): lax.psum(partial_value.astype(jnp.bfloat16), 'lat').astype(jnp.float32)  62.3 us
    psum x1, blocking collectives, body(): totals, norm_totals = lax.psum((squares, norm_vector), ('layer', 'lat'))  41.5 us
    gather x1, local copies, waits for them, and re-layouts, body(): picked = jnp.take(shard_rows, clipped, axis=0)  24.4 us
    gather x4, local copies, waits for them, and re-layouts, body(): preact = (products - shifts[clipped]) / picked_norms + enc_bias[0][clipped]  23.6 us
    dot_general x1, matrix products, body(): jnp.dot(shard_rows, dec_bias[0], precision=lax.Precision.HIGHEST, preferr...  13 us
    scatter-add x1, other arithmetic, body(): jnp.zeros((lat_dev,), jnp.float32).at[clipped.reshape(-1)]  11.9 us
    gather x2, local copies, waits for them, and re-layouts, body(): picked_norms = row_norms[clipped]  11.8 us
    dot_general x1, matrix products, body(): jnp.einsum('ct,ctd->td', coefficient, picked, preferred_element_type=jnp....  9.84 us
  transfers between devices with their start and end apart: 6, of which 4 were waited for; matrix products, arithmetic and copies ran while one was open for 37% of the time, Pallas kernels for 0%

commit v1 on v0

v1 whole, which is shorter than its diff:
```python
import functools
import jax
import jax.numpy as jnp
from jax import lax
from jax.experimental import pallas as pl
from jax.experimental.pallas import tpu as pltpu
from jax.sharding import PartitionSpec as P

F32 = jnp.float32
BF16 = jnp.bfloat16
LOW = 64
VMEM_SPEC = pl.BlockSpec(memory_space=pltpu.VMEM)
SMEM_SPEC = pl.BlockSpec(memory_space=pltpu.SMEM)


def split_lat(count):
    inner = 1
    while inner * inner * 4 <= count and count % (inner * 2) == 0:
        inner *= 2
    return count // inner, inner


def shift_to(value, axis, size, mask):
    return lax.ppermute(value, axis, [(i, i ^ mask) for i in range(size)])


def pack_kernel(groups, per_shard, lat_dev, group_ref, res_ref, slots_ref, *outs):
    group = group_ref[0]
    width = res_ref.shape[2]
    slot_count = slots_ref.shape[2]
    shard = lax.broadcasted_iota(jnp.int32, slots_ref.shape[1:], 1) // per_shard
    for mask in range(groups):
        layer = jnp.bitwise_xor(group, mask)
        slots = slots_ref[layer]
        live = slots >= 0
        local = slots - shard * lat_dev
        high = jnp.where(live, local // LOW, -1)
        low = jnp.where(live, local % LOW, 0)
        outs[mask][:, :width] = res_ref[layer]
        outs[mask][:, width : width + 2 * slot_count] = jnp.concatenate([high, low], axis=1).astype(F32).astype(BF16)


def pack(group, residuals, slots, per_shard, lat_dev):
    groups, rows, width = residuals.shape
    out = jax.ShapeDtypeStruct((rows, width + 2 * slots.shape[2]), BF16)
    return pl.pallas_call(
        functools.partial(pack_kernel, groups, per_shard, lat_dev),
        out_shape=[out] * groups,
        in_specs=[SMEM_SPEC, VMEM_SPEC, VMEM_SPEC],
        out_specs=[VMEM_SPEC] * groups,
        name="pack",
    )(group, residuals, slots)


def norms_kernel(dict_ref, enc_ref, dec_ref, cols_ref, total_ref):
    rows = dict_ref.shape[0]
    tile = dict_ref[...].astype(F32)
    squares = jnp.sum(tile * tile, axis=1, keepdims=True)
    shift = jnp.sum(tile * dec_ref[...], axis=1, keepdims=True)
    norm = jnp.sqrt(squares + 1e-06)
    inverse = 1.0 / norm
    eye = lax.broadcasted_iota(jnp.int32, (128, 128), 0) == lax.broadcasted_iota(jnp.int32, (128, 128), 1)
    enc = jnp.concatenate(
        [
            jnp.sum(jnp.where(eye, enc_ref[:, k * 128 : (k + 1) * 128], 0.0), axis=1, keepdims=True)
            for k in range(rows // 128)
        ],
        axis=0,
    )
    offset = enc - shift * inverse
    lane = lax.broadcasted_iota(jnp.int32, (rows, 128), 1)
    cols_ref[...] = jnp.where(lane == 0, inverse, offset)

    @pl.when(pl.program_id(0) == 0)
    def _():
        total_ref[...] = jnp.zeros_like(total_ref)

    total_ref[...] += jnp.sum(norm)


def norms(dictionary, enc_bias, dec_bias, tile):
    lat_dev, width = dictionary.shape
    return pl.pallas_call(
        norms_kernel,
        grid=(lat_dev // tile,),
        out_shape=[
            jax.ShapeDtypeStruct((lat_dev, 128), F32),
            jax.ShapeDtypeStruct((8, 128), F32),
        ],
        in_specs=[
            pl.BlockSpec((tile, width), lambda i: (i, 0)),
            pl.BlockSpec((1, tile), lambda i: (0, i)),
            pl.BlockSpec((1, width), lambda i: (0, 0)),
        ],
        out_specs=[
            pl.BlockSpec((tile, 128), lambda i: (i, 0)),
            pl.BlockSpec((8, 128), lambda i: (0, 0)),
        ],
        name="norms",
    )(dictionary, enc_bias, dec_bias)


def main_kernel(blocks, per_shard, slot_count, r_dev, shard_ref, seed_ref, dict_ref, cols_ref, *refs):
    ins = refs[:blocks]
    shares = refs[blocks : 2 * blocks]
    normed_out, own_ref, mass_ref = refs[2 * blocks : 2 * blocks + 3]
    normed, ids, weights, estimate = refs[2 * blocks + 3 :]
    step = pl.program_id(0)
    tile, width = dict_ref.shape
    rows = ins[0].shape[0]
    tokens = rows * blocks

    @pl.when(step == 0)
    def _():
        total = jnp.zeros((1, 1), F32)
        for block in ins:
            raw = block[:, :width].astype(F32)
            total += jnp.sum(raw * raw, keepdims=True)
        scale = lax.rsqrt(total / (tokens * width))
        for k, block in enumerate(ins):
            normed[k * rows : (k + 1) * rows, :] = (block[:, :width].astype(F32) * scale).astype(BF16)
        coded = jnp.concatenate([block[:, width:] for block in ins], axis=0)
        slot = lax.broadcasted_iota(jnp.int32, (per_shard, 2 * slot_count), 0) + shard_ref[0] * per_shard
        column = lax.broadcasted_iota(jnp.int32, (per_shard, 2 * slot_count), 1)
        pick = lambda shift: lax.dot_general(
            jnp.where(column == slot + shift, 1.0, 0.0).astype(BF16),
            coded,
            (((1,), (1,)), ((), ())),
            preferred_element_type=F32,
        )
        ids_now = pick(0) * LOW + pick(slot_count)
        ids[...] = ids_now
        weights[...] = sum(jnp.where(ids_now == ids_now[c : c + 1], 1.0, 0.0) for c in range(per_shard))
        estimate[...] = jnp.zeros_like(estimate)

    products = lax.dot_general(
        dict_ref[...], normed[...], (((1,), (1,)), ((), ())), preferred_element_type=F32
    )
    latent = (lax.broadcasted_iota(jnp.int32, (tile, tokens), 0) + step * tile).astype(F32)
    count = jnp.zeros((tile, tokens), F32)
    for c in range(per_shard):
        count = jnp.where(latent == ids[c : c + 1, :], weights[c : c + 1, :], count)
    inverse = cols_ref[:, 0:1]
    activity = jnp.maximum(products * inverse + cols_ref[:, 1:2], 0.0)
    eye = lax.broadcasted_iota(jnp.int32, (128, 128), 0) == lax.broadcasted_iota(jnp.int32, (128, 128), 1)
    mass = jnp.sum(activity * count, axis=1, keepdims=True)
    for k in range(tile // 128):
        mass_ref[:, k * 128 : (k + 1) * 128] = jnp.sum(
            jnp.where(eye, mass[k * 128 : (k + 1) * 128], 0.0), axis=0, keepdims=True
        )
    coefficient = (activity * inverse).astype(BF16) * count.astype(BF16)
    estimate[...] += lax.dot_general(
        coefficient, dict_ref[...], (((0,), (0,)), ((), ())), preferred_element_type=F32
    )

    @pl.when(step == pl.num_programs(0) - 1)
    def _():
        share = estimate[...].astype(BF16)
        place = lax.broadcasted_iota(jnp.int32, (tokens, r_dev * blocks), 0)
        chosen = jnp.where(place == seed_ref[...], 1.0, 0.0).astype(BF16)
        seeds = lax.dot_general(chosen, share, (((0,), (0,)), ((), ())), preferred_element_type=F32).astype(BF16)
        seed_features = lax.dot_general(
            chosen, normed[...], (((0,), (0,)), ((), ())), preferred_element_type=F32
        ).astype(BF16)
        for k in range(blocks):
            shares[k][:rows] = share[k * rows : (k + 1) * rows]
            shares[k][rows:] = seeds[k * r_dev : (k + 1) * r_dev]
        own_ref[:rows] = normed[:rows]
        own_ref[rows:] = seed_features[:r_dev]
        normed_out[...] = normed[...]


def main(shard, seed_places, dictionary, cols, blocks, per_shard, slot_count, tile):
    lat_dev, width = dictionary.shape
    count = len(blocks)
    rows = blocks[0].shape[0]
    tokens = rows * count
    r_dev = seed_places.shape[1] // count
    share = jax.ShapeDtypeStruct((rows + r_dev, width), BF16)
    whole = lambda shape: pl.BlockSpec(shape, lambda i: (0,) * len(shape))
    return pl.pallas_call(
        functools.partial(main_kernel, count, per_shard, slot_count, r_dev),
        grid=(lat_dev // tile,),
        out_shape=[share] * count
        + [
            jax.ShapeDtypeStruct((tokens, width), BF16),
            share,
            jax.ShapeDtypeStruct((1, lat_dev), F32),
        ],
        in_specs=[
            SMEM_SPEC,
            whole(seed_places.shape),
            pl.BlockSpec((tile, width), lambda i: (i, 0)),
            pl.BlockSpec((tile, 128), lambda i: (i, 0)),
        ]
        + [whole(blocks[0].shape)] * count,
        out_specs=[whole(share.shape)] * count
        + [
            whole((tokens, width)),
            whole(share.shape),
            pl.BlockSpec((1, tile), lambda i: (0, i)),
        ],
        scratch_shapes=[
            pltpu.VMEM((tokens, width), BF16),
            pltpu.VMEM((per_shard, tokens), F32),
            pltpu.VMEM((per_shard, tokens), F32),
            pltpu.VMEM((tokens, width), F32),
        ],
        name="sparse_code",
    )(shard, seed_places, dictionary, cols, *blocks)


def finish_kernel(parts, groups, latents, own_ref, dec_ref, norm_ref, *refs):
    shares = refs[:parts]
    recon = refs[parts : parts + groups]
    rows_ref, numerator_ref = refs[parts + groups :]
    r_dev = rows_ref.shape[0]
    rows = own_ref.shape[0] - r_dev
    summed = shares[0][...].astype(F32)
    for share in shares[1:]:
        summed += share[...].astype(F32)
    estimate = summed + dec_ref[...]
    errors = own_ref[...].astype(F32) - estimate
    size = rows // groups
    for k in range(groups):
        recon[k][...] = estimate[k * size : (k + 1) * size].astype(BF16)
    own = errors[:rows]
    numerator_ref[...] = jnp.full(numerator_ref.shape, jnp.sum(own * own), F32)
    seeds = errors[rows:]
    norm = jnp.sqrt(jnp.sum(seeds * seeds, axis=1, keepdims=True) + 1e-06)
    rows_ref[...] = (seeds / norm * (norm_ref[0:1, 0:1] / latents)).astype(BF16)


def finish(shares, own, dec_bias, norm_total, groups, r_dev, latents):
    rows = own.shape[0] - r_dev
    width = own.shape[1]
    return pl.pallas_call(
        functools.partial(finish_kernel, len(shares), groups, latents),
        out_shape=[jax.ShapeDtypeStruct((rows // groups, width), BF16)] * groups
        + [jax.ShapeDtypeStruct((r_dev, width), BF16), jax.ShapeDtypeStruct((8, 128), F32)],
        in_specs=[VMEM_SPEC] * (3 + len(shares)),
        out_specs=[VMEM_SPEC] * (groups + 2),
        name="finish",
    )(own, dec_bias, norm_total, *shares)


def all_sum(value, axis, size):
    mask = 1
    while mask < size:
        value = value + shift_to(value, axis, size, mask)
        mask *= 2
    return value


def body(residuals, topk_slots, dictionary, enc_bias, dec_bias, dead_ids, seed_tokens):
    tok_dev = residuals.shape[1]
    lat_count = lax.axis_size("lat")
    groups = lax.axis_size("layer")
    shard = lax.axis_index("lat")
    group = lax.axis_index("layer")
    lat_dev = dictionary.shape[1]
    slot_count = topk_slots.shape[2]
    per_shard = slot_count // lat_count
    r_dev = seed_tokens.shape[1] // lat_count
    outer, inner = split_lat(lat_count)

    packed = pack(group.reshape(1), residuals, topk_slots, per_shard, lat_dev)
    mine = jnp.concatenate(
        [packed[0]] + [shift_to(packed[k], "layer", groups, k) for k in range(1, groups)], axis=0
    )

    columns = [mine] + [shift_to(mine, "lat", lat_count, inner * z) for z in range(1, outer)]
    blocks = [
        block
        for column in columns
        for block in [column] + [shift_to(column, "lat", lat_count, x) for x in range(1, inner)]
    ]

    cols, norm_part = norms(dictionary[0], enc_bias, dec_bias, 512)
    norm_total = all_sum(norm_part, "lat", lat_count)

    unit = seed_tokens[0] // tok_dev
    tok_group = tok_dev * groups
    place = (
        jnp.bitwise_xor(unit % lat_count, shard) * tok_group
        + jnp.bitwise_xor(unit // lat_count, group) * tok_dev
        + seed_tokens[0] % tok_dev
    )
    order = jnp.bitwise_xor(jnp.arange(lat_count), shard)
    place = place.reshape(lat_count, r_dev)[order].reshape(1, -1)

    results = main(shard.reshape(1), place, dictionary[0], cols, blocks, per_shard, slot_count, 512)
    shares = results[:lat_count]
    normed, own, mass = results[lat_count:]

    sums = [None] * outer
    for z in reversed(range(outer)):
        total = shares[z * inner].astype(F32)
        for x in range(1, inner):
            total = total + shift_to(shares[z * inner + x], "lat", lat_count, x).astype(F32)
        sums[z] = total
    final = [sums[0]] + [shift_to(sums[z].astype(BF16), "lat", lat_count, inner * z) for z in range(1, outer)]

    *recon, new_rows, numerator = finish(final, own, dec_bias, norm_total, groups, r_dev, lat_dev * lat_count)
    numerator = all_sum(numerator, "lat", lat_count)[0, 0]
    returned = jnp.stack([recon[0]] + [shift_to(recon[k], "layer", groups, k) for k in range(1, groups)])
    reconstruction = returned[jnp.bitwise_xor(jnp.arange(groups), group)]

    feat32 = normed.astype(F32)
    centered = feat32 - jnp.mean(feat32, axis=0)
    unexplained = (numerator / jnp.sum(jnp.square(centered))).reshape(1)
    candidates = shard * lat_dev + jnp.arange(lat_dev, dtype=jnp.int32)
    is_dead = jnp.any(dead_ids[0][:, None] == candidates[None, :], axis=0)
    new_bias = jnp.where(is_dead, 0.0, enc_bias[0])[None]
    return (reconstruction, unexplained, mass, new_rows[None], new_bias)


def solution(mesh):
    in_specs = (
        P(None, ("layer", "lat"), None),
        P(None, ("layer", "lat"), None),
        P("layer", "lat", None),
        P("layer", "lat"),
        P("layer", None),
        P("layer", None),
        P("layer", None),
    )
    out_specs = (
        P(None, ("layer", "lat"), None),
        P("layer"),
        P("layer", "lat"),
        P("layer", "lat", None),
        P("layer", "lat"),
    )
    return jax.shard_map(body, mesh=mesh, in_specs=in_specs, out_specs=out_specs, check_vma=False)
```

time: 292 us -> 119 us (0.41)
  local copies, waits for them, and re-layouts: 69 us -> 4.82 us
  Pallas kernels: 0 us -> 43.9 us
  waiting for transfers between devices: 73.1 us -> 29.5 us
  blocking collectives: 41.5 us -> 0 us
  matrix products: 32.6 us -> 0 us
  other arithmetic: 41.2 us -> 9.74 us
  between operations: 17.4 us -> 3.23 us
  starting transfers between devices: 16.5 us -> 27.4 us
    psum x1 -> x0, waiting for transfers between devices: 62.3 us -> none  [body(): lax.psum(partial_value.astype(jnp.bfloat16), 'lat').astype(jnp.float32)]
    gather x8 -> x2, local copies, waits for them, and re-layouts: 60.4 us -> 1.76 us  [the longest x1 1.21 us: body(): reconstruction = returned[jnp.bitwise_xor(jnp.arange(groups), group)]]
    pallas_call x0 -> x4, Pallas kernels: none -> 43.9 us  [the longest x1 26.9 us: main(): pl.pallas_call(functools.partial(main_kernel, count, per_shard, slot_coun...]
    psum x1 -> x0, blocking collectives: 41.5 us -> none  [body(): totals, norm_totals = lax.psum((squares, norm_vector), ('layer', 'lat'))]
    dot_general x3 -> x0, matrix products: 32.6 us -> none  [the longest x1 13 us: body(): jnp.dot(shard_rows, dec_bias[0], precision=lax.Precision.HIGHEST, preferr...]
    ppermute x0 -> x26, waiting for transfers between devices: none -> 29.5 us  [shift_to(): return lax.ppermute(value, axis, [(i, i ^ mask) for i in range(size)])]
    ppermute x0 -> x26, starting transfers between devices: none -> 27.4 us  [shift_to(): return lax.ppermute(value, axis, [(i, i ^ mask) for i in range(size)])]
    all_to_all x4 -> x0, starting transfers between devices: 16.2 us -> none  [the longest x1 5.31 us: body(): lax.all_to_all(lax.all_to_all(topk_slots, 'layer', split_axis=0, concat_a...]
  transfers between devices with their start and end apart: 6 -> 26, of which waited for: 4 -> 11; matrix products, arithmetic and copies ran while one was open for 37% -> 10% of each run, Pallas kernels for 0% -> 34%
where the time goes in v1:
time: 119 us
  Pallas kernels  43.9 us (37%)
  waiting for transfers between devices  29.5 us (25%)
  starting transfers between devices  27.4 us (23%)
  other arithmetic  9.74 us (8%)
  local copies, waits for them, and re-layouts  4.82 us (4%)
  between operations  3.23 us (3%)
    ppermute x26, waiting for transfers between devices, shift_to(): return lax.ppermute(value, axis, [(i, i ^ mask) for i in range(size)])  29.5 us
    ppermute x26, starting transfers between devices, shift_to(): return lax.ppermute(value, axis, [(i, i ^ mask) for i in range(size)])  27.4 us
    pallas_call x1, Pallas kernels, main(): pl.pallas_call(functools.partial(main_kernel, count, per_shard, slot_coun...  26.9 us
    pallas_call x1, Pallas kernels, norms(): pl.pallas_call(norms_kernel, grid=(lat_dev // tile,), out_shape=[jax.Shap...  13.1 us
    convert_element_type x3, other arithmetic, body(): sums[z].astype(BF16)  2.93 us
  transfers between devices with their start and end apart: 26, of which 11 were waited for; matrix products, arithmetic and copies ran while one was open for 10% of the time, Pallas kernels for 34%

profile of v1, /device:TPU:0, one launch (start us, length us, event | category | flops | bytes accessed | tf_op | source)
XLA Modules:
  0.0 118.6 jit_solution(3073628253086812715)
XLA Ops:
  0.6 1.6 %pack.1 = (bf16[8,2176]{1,0:T(8,128)(2,1)}, bf16[8,2176]{1,0:T(8,128)(2,1)}, bf16[8,2176]{1,0:T(8,128)(2,1)}, bf16[8,2176]{1,0:T(8,128)(2,1)}) custom-call(s32[1]{0:T(128)} %bitcast.3.group_ref, bf16[4,8,2048]{2,1,0:T(8,128)(2,1)} %res_ref.1, s32[4,8,64]{2,1,0:T(8,128)} %slots_ref.1), custom_call_target="tpu_custom_call" | custom-call | tf_op jit(solution)/shard_map/pack/pallas_call | solution.py:46
  2.3 0.5 collective-permute-start
  2.8 2.5 %collective-permute-start.1 = (bf16[8,2176]{1,0:T(8,128)(2,1)}, bf16[8,2176]{1,0:T(8,128)(2,1)S(1)}, u32[]{:S(2)}, u32[]{:S(2)}) collective-permute-start(bf16[8,2176]{1,0:T(8,128)(2,1)} %get-tuple-element.31), channel_id=1, source_target_pairs={{0,16},{8,24},{16,0},{24,8},{1,17},{9,25},{17,1},{25,9},{2,18},{10... | collective-permute-start | bytes 104456 | tf_op jit(solution)/shard_map/ppermute | solution.py:24
  5.3 0.1 collective-permute-start.2
  5.4 13.1 %norms.1 = (f32[4096,128]{1,0:T(8,128)}, f32[8,128]{1,0:T(8,128)}) custom-call(bf16[4096,2048]{1,0:T(8,128)(2,1)} %bitcast.15, f32[1,4096]{1,0:T(1,128)} %enc_ref.1, f32[1,2048]{1,0:T(1,128)} %dec_ref.3), custom_call_target="tpu_custom_call" | custom-call | tf_op jit(solution)/shard_map/norms/pallas_call | solution.py:83
  18.5 1.7 %collective-permute-start.10 = (f32[8,128]{1,0:T(8,128)}, f32[8,128]{1,0:T(8,128)S(1)}, u32[]{:S(2)}, u32[]{:S(2)}) collective-permute-start(f32[8,128]{1,0:T(8,128)} %get-tuple-element.34), channel_id=1, source_target_pairs={{0,1},{1,0},{2,3},{3,2},{4,5},{5,4},{6,7},{7,6},{8,9},{9,8},{10,11... | collective-permute-start | bytes 12296 | tf_op jit(solution)/shard_map/ppermute | solution.py:24
  20.3 0.3 compare_reduce_fusion
  20.6 0.6 reshape_select_fusion
  21.3 0.5 broadcast.130
  21.8 0.7 reduce.3
  22.4 0.1 squeeze.12
  22.5 0.0 collective-permute-done
  22.5 0.0 collective-permute-done.1
  22.6 0.0 collective-permute-done.2
  22.6 1.6 %collective-permute-start.4 = (bf16[32,2176]{1,0:T(8,128)(2,1)S(1)}, bf16[32,2176]{1,0:T(8,128)(2,1)S(1)}, u32[]{:S(2)}, u32[]{:S(2)}) collective-permute-start(bf16[32,2176]{1,0:T(8,128)(2,1)S(1)} %constant_dynamic-update-slice_fusion.refs_0_), channel_id=1, source_target_pairs={{0,2},{1,3},{2,0},{3,1},{4,6},{5,7},{6,4},{7,5},{8,10},{9,11},{10,... | collective-permute-start | bytes 417800 | tf_op jit(solution)/shard_map/ppermute | solution.py:24
  24.2 2.6 %collective-permute-start.6 = (bf16[32,2176]{1,0:T(8,128)(2,1)S(1)}, bf16[32,2176]{1,0:T(8,128)(2,1)S(1)}, u32[]{:S(2)}, u32[]{:S(2)}) collective-permute-start(bf16[32,2176]{1,0:T(8,128)(2,1)S(1)} %constant_dynamic-update-slice_fusion.refs_0_), channel_id=1, source_target_pairs={{0,4},{1,5},{2,6},{3,7},{4,0},{5,1},{6,2},{7,3},{8,12},{9,13},{10,... | collective-permute-start | bytes 417800 | tf_op jit(solution)/shard_map/ppermute | solution.py:24
  26.8 0.2 collective-permute-start.8
  27.1 0.4 collective-permute-start.3
  27.5 2.8 %collective-permute-done.4.refs_2_ = bf16[32,2176]{1,0:T(8,128)(2,1)S(1)} collective-permute-done((bf16[32,2176]{1,0:T(8,128)(2,1)S(1)}, bf16[32,2176]{1,0:T(8,128)(2,1)S(1)}, u32[]{:S(2)}, u32[]{:S(2)}) %collective-permute-start.4) | collective-permute-done | bytes 139296 | tf_op jit(solution)/shard_map/ppermute | solution.py:24
  30.3 0.3 collective-permute-start.5
  30.6 7.1 %collective-permute-done.6.refs_4_ = bf16[32,2176]{1,0:T(8,128)(2,1)S(1)} collective-permute-done((bf16[32,2176]{1,0:T(8,128)(2,1)S(1)}, bf16[32,2176]{1,0:T(8,128)(2,1)S(1)}, u32[]{:S(2)}, u32[]{:S(2)}) %collective-permute-start.6) | collective-permute-done | bytes 139296 | tf_op jit(solution)/shard_map/ppermute | solution.py:24
  37.7 0.5 collective-permute-start.7
  38.2 0.0 collective-permute-done.8.refs_6_
  38.2 1.5 %collective-permute-start.9 = (bf16[32,2176]{1,0:T(8,128)(2,1)S(1)}, bf16[32,2176]{1,0:T(8,128)(2,1)S(1)}, u32[]{:S(2)}, u32[]{:S(2)}) collective-permute-start(bf16[32,2176]{1,0:T(8,128)(2,1)S(1)} %collective-permute-done.8.refs_6_), channel_id=1, source_target_pairs={{0,1},{1,0},{2,3},{3,2},{4,5},{5,4},{6,7},{7,6},{8,9},{9,8},{10,11... | collective-permute-start | bytes 417800 | tf_op jit(solution)/shard_map/ppermute | solution.py:24
  39.7 0.6 gather_fusion
  40.3 0.6 reshape.66.seed_ref
  40.9 0.7 add.89
  41.5 0.9 collective-permute-start.11
  42.4 0.3 collective-permute-done.7.refs_5_
  42.7 1.5 %collective-permute-done.9.refs_7_ = bf16[32,2176]{1,0:T(8,128)(2,1)S(1)} collective-permute-done((bf16[32,2176]{1,0:T(8,128)(2,1)S(1)}, bf16[32,2176]{1,0:T(8,128)(2,1)S(1)}, u32[]{:S(2)}, u32[]{:S(2)}) %collective-permute-start.9) | collective-permute-done | bytes 139296 | tf_op jit(solution)/shard_map/ppermute | solution.py:24
  44.3 0.6 copy-done.11
  44.9 26.9 %sparse_code.1 = (bf16[48,2048]{1,0:T(8,128)(2,1)}, bf16[48,2048]{1,0:T(8,128)(2,1)}, bf16[48,2048]{1,0:T(8,128)(2,1)}, bf16[48,2048]{1,0:T(8,128)(2,1)}, bf16[4...) custom-call(s32[1]{0:T(128)} %bitcast.shard_ref, ...), custom_call_target="tpu_custom_call" | custom-call | tf_op jit(solution)/shard_map/sparse_code/pallas_call | solution.py:181
  71.8 0.6 collective-permute-start.18
  72.4 1.9 %collective-permute-start.12 = (f32[8,128]{1,0:T(8,128)S(1)}, f32[8,128]{1,0:T(8,128)S(1)}, u32[]{:S(2)}, u32[]{:S(2)}) collective-permute-start(f32[8,128]{1,0:T(8,128)S(1)} %add.90), channel_id=1, source_target_pairs={{0,4},{1,5},{2,6},{3,7},{4,0},{5,1},{6,2},{7,3},{8,12},{9,13},{10,... | collective-permute-start | bytes 12296 | tf_op jit(solution)/shard_map/ppermute | solution.py:24
  74.4 2.6 %collective-permute-done.12 = f32[8,128]{1,0:T(8,128)S(1)} collective-permute-done((f32[8,128]{1,0:T(8,128)S(1)}, f32[8,128]{1,0:T(8,128)S(1)}, u32[]{:S(2)}, u32[]{:S(2)}) %collective-permute-start.12) | collective-permute-done | bytes 4128 | tf_op jit(solution)/shard_map/ppermute | solution.py:24
  77.0 0.6 add.91.norm_ref
  77.6 1.5 %collective-permute-start.16 = (bf16[48,2048]{1,0:T(8,128)(2,1)}, bf16[48,2048]{1,0:T(8,128)(2,1)S(1)}, u32[]{:S(2)}, u32[]{:S(2)}) collective-permute-start(bf16[48,2048]{1,0:T(8,128)(2,1)} %get-tuple-element.40), channel_id=1, source_target_pairs={{0,1},{1,0},{2,3},{3,2},{4,5},{5,4},{6,7},{7,6},{8,9},{9,8},{10,11... | collective-permute-start | bytes 589832 | tf_op jit(solution)/shard_map/ppermute | solution.py:24
  79.1 0.5 collective-permute-start.14
  79.6 1.5 %collective-permute-start.13 = (bf16[48,2048]{1,0:T(8,128)(2,1)}, bf16[48,2048]{1,0:T(8,128)(2,1)S(1)}, u32[]{:S(2)}, u32[]{:S(2)}) collective-permute-start(bf16[48,2048]{1,0:T(8,128)(2,1)} %get-tuple-element.36), channel_id=1, source_target_pairs={{0,1},{1,0},{2,3},{3,2},{4,5},{5,4},{6,7},{7,6},{8,9},{9,8},{10,11... | collective-permute-start | bytes 589832 | tf_op jit(solution)/shard_map/ppermute | solution.py:24
  81.1 1.0 add_convert_fusion
  82.1 2.4 %collective-permute-start.19 = (bf16[48,2048]{1,0:T(8,128)(2,1)S(1)}, bf16[48,2048]{1,0:T(8,128)(2,1)S(1)}, u32[]{:S(2)}, u32[]{:S(2)}) collective-permute-start(bf16[48,2048]{1,0:T(8,128)(2,1)S(1)} %add_convert_fusion), channel_id=1, source_target_pairs={{0,6},{1,7},{2,4},{3,5},{4,2},{5,3},{6,0},{7,1},{8,14},{9,15},{10,... | collective-permute-start | bytes 589832 | tf_op jit(solution)/shard_map/ppermute | solution.py:24
  84.5 1.1 collective-permute-done.16
  85.6 1.0 add_convert_fusion.1
  86.6 1.9 %collective-permute-start.17 = (bf16[48,2048]{1,0:T(8,128)(2,1)S(1)}, bf16[48,2048]{1,0:T(8,128)(2,1)S(1)}, u32[]{:S(2)}, u32[]{:S(2)}) collective-permute-start(bf16[48,2048]{1,0:T(8,128)(2,1)S(1)} %add_convert_fusion.1), channel_id=1, source_target_pairs={{0,4},{1,5},{2,6},{3,7},{4,0},{5,1},{6,2},{7,3},{8,12},{9,13},{10,... | collective-permute-start | bytes 589832 | tf_op jit(solution)/shard_map/ppermute | solution.py:24
  88.5 1.0 add_convert_fusion.2
  89.5 1.1 collective-permute-start.15
  90.6 1.7 %convert_add_fusion.refs_0_ = f32[48,2048]{1,0:T(8,128)} fusion(bf16[48,2048]{1,0:T(8,128)(2,1)S(1)} %collective-permute-done.13, bf16[48,2048]{1,0:T(8,128)(2,1)} %get-tuple-element.35), kind=kLoop, calls=%fused_computation.10 | loop fusion | flops 294912 | bytes 786432 | tf_op jit(solution)/shard_map/add | solution.py:300
  92.3 6.0 %collective-permute-done.17.refs_2_ = bf16[48,2048]{1,0:T(8,128)(2,1)S(1)} collective-permute-done((bf16[48,2048]{1,0:T(8,128)(2,1)S(1)}, bf16[48,2048]{1,0:T(8,128)(2,1)S(1)}, u32[]{:S(2)}, u32[]{:S(2)}) %collective-permute-start.17) | collective-permute-done | bytes 196640 | tf_op jit(solution)/shard_map/ppermute | solution.py:24
  98.4 0.5 collective-permute-done.15.refs_1_
  98.9 0.1 copy-done.3
  99.0 0.5 copy-done.4
  99.6 2.2 %finish.1 = (bf16[8,2048]{1,0:T(8,128)(2,1)}, bf16[8,2048]{1,0:T(8,128)(2,1)}, bf16[8,2048]{1,0:T(8,128)(2,1)}, bf16[8,2048]{1,0:T(8,128)(2,1)}, bf16[16,2048]{1,0:T(8,128)(2,1)}, /*index=5*/f32[8,128]{1,0:T(8,128)}) custom-call(bf16[48,2048]{1,0:T(8,128)(2,1)} %get-tuple-element.33.own_ref, f32[1,2048]{1,0:T(1,128)} %dec_ref.3, f32[8,128]{1,0:T(8,128)} %add.91.norm_ref, ...), custom_call_target="tpu_custom_call" | custom-call | tf_op jit(solution)/shard_map/finish/pallas_call | solution.py:237
  101.8 0.6 collective-permute-start.23
  102.4 0.2 convert_reduce_fusion
  102.6 3.0 %collective-permute-done.23 = f32[8,128]{1,0:T(8,128)S(1)} collective-permute-done((f32[8,128]{1,0:T(8,128)}, f32[8,128]{1,0:T(8,128)S(1)}, u32[]{:S(2)}, u32[]{:S(2)}) %collective-permute-start.23) | collective-permute-done | bytes 4128 | tf_op jit(solution)/shard_map/ppermute | solution.py:24
  105.6 0.7 add.97
  106.3 1.6 %collective-permute-start.21 = (bf16[8,2048]{1,0:T(8,128)(2,1)}, bf16[8,2048]{1,0:T(8,128)(2,1)S(1)}, u32[]{:S(2)}, u32[]{:S(2)}) collective-permute-start(bf16[8,2048]{1,0:T(8,128)(2,1)} %get-tuple-element.45), channel_id=1, source_target_pairs={{0,16},{8,24},{16,0},{24,8},{1,17},{9,25},{17,1},{25,9},{2,18},{10... | collective-permute-start | bytes 98312 | tf_op jit(solution)/shard_map/ppermute | solution.py:24
  107.9 0.3 collective-permute-start.22
  108.1 1.7 %collective-permute-done.24 = f32[8,128]{1,0:T(8,128)S(1)} collective-permute-done((f32[8,128]{1,0:T(8,128)S(1)}, f32[8,128]{1,0:T(8,128)S(1)}, u32[]{:S(2)}, u32[]{:S(2)}) %collective-permute-start.24) | collective-permute-done | bytes 4128 | tf_op jit(solution)/shard_map/ppermute | solution.py:24
  109.9 0.5 collective-permute-start.25
  110.4 1.2 %fusion.1 = f32[]{:T(128)} fusion(bf16[256,2048]{1,0:T(8,128)(2,1)S(1)} %copy-done, f32[2048]{0:T(1024)S(1)} %broadcast_multiply_fusion), kind=kLoop, calls=%fused_computation.5 | loop fusion | flops 2097151 | bytes 1056772 | tf_op jit(solution)/shard_map/reduce_sum | solution.py:311
  111.6 2.8 %collective-permute-done.25 = f32[8,128]{1,0:T(8,128)S(1)} collective-permute-done((f32[8,128]{1,0:T(8,128)S(1)}, f32[8,128]{1,0:T(8,128)S(1)}, u32[]{:S(2)}, u32[]{:S(2)}) %collective-permute-start.25) | collective-permute-done | bytes 4128 | tf_op jit(solution)/shard_map/ppermute | solution.py:24
  114.4 0.5 slice.3
  116.2 1.2 %gather_fusion.1 = bf16[4,8,2048]{2,1,0:T(8,128)(2,1)} fusion(bf16[4,8,2048]{2,1,0:T(8,128)(2,1)S(1)} %pad_maximum_fusion, s32[1024]{0:T(1024)S(1)} %pad_clamp_fusion), kind=kCustom, calls=%fused_computation.1 | custom fusion | bytes 262160 | tf_op jit(solution)/shard_map/gather | solution.py:307
  (59 shorter events, 0.2 us)
Async XLA Ops:
  2.3 20.2 %collective-permute-start = (bf16[8,2176]{1,0:T(8,128)(2,1)}, bf16[8,2176]{1,0:T(8,128)(2,1)S(1)}, u32[]{:S(2)}, u32[]{:S(2)}) collective-permute-start(bf16[8,2176]{1,0:T(8,128)(2,1)} %get-tuple-element.30), channel_id=1, source_target_pairs={{0,8},{8,0},{16,24},{24,16},{1,9},{9,1},{17,25},{25,17},{2,10},{10... | collective-permute-start | bytes 104456 | tf_op jit(solution)/shard_map/ppermute | solution.py:24
  2.8 19.8 %collective-permute-start.1 = (bf16[8,2176]{1,0:T(8,128)(2,1)}, bf16[8,2176]{1,0:T(8,128)(2,1)S(1)}, u32[]{:S(2)}, u32[]{:S(2)}) collective-permute-start(bf16[8,2176]{1,0:T(8,128)(2,1)} %get-tuple-element.31), channel_id=1, source_target_pairs={{0,16},{8,24},{16,0},{24,8},{1,17},{9,25},{17,1},{25,9},{2,18},{10... | collective-permute-start | bytes 104456 | tf_op jit(solution)/shard_map/ppermute | solution.py:24
  5.3 17.3 %collective-permute-start.2 = (bf16[8,2176]{1,0:T(8,128)(2,1)}, bf16[8,2176]{1,0:T(8,128)(2,1)S(1)}, u32[]{:S(2)}, u32[]{:S(2)}) collective-permute-start(bf16[8,2176]{1,0:T(8,128)(2,1)} %get-tuple-element.32), channel_id=1, source_target_pairs={{0,24},{8,16},{16,8},{24,0},{1,25},{9,17},{17,9},{25,1},{2,26},{10... | collective-permute-start | bytes 104456 | tf_op jit(solution)/shard_map/ppermute | solution.py:24
  5.4 14.9 %copy-start.15 = (s32[1,128]{1,0:T(1,128)S(1)}, s32[1,128]{1,0:T(1,128)}, u32[]{:S(2)}) copy-start(s32[1,128]{1,0:T(1,128)} %param.12) | copy-start | bytes 1540
  5.4 15.2 %copy-start.12 = (f32[1,4096]{1,0:T(1,128)S(1)}, f32[1,4096]{1,0:T(1,128)}, u32[]{:S(2)}) copy-start(f32[1,4096]{1,0:T(1,128)} %enc_ref.1) | copy-start | bytes 49156
  5.4 15.9 %copy-start.13 = (bf16[8,2176]{1,0:T(8,128)(2,1)S(1)}, bf16[8,2176]{1,0:T(8,128)(2,1)}, u32[]{:S(2)}) copy-start(bf16[8,2176]{1,0:T(8,128)(2,1)} %get-tuple-element.29) | copy-start | bytes 104452
  5.4 16.4 %copy-start.16 = (s32[1,128]{1,0:T(1,128)S(1)}, s32[1,128]{1,0:T(1,128)}, u32[]{:S(2)}) copy-start(s32[1,128]{1,0:T(1,128)} %param.13) | copy-start | bytes 1540
  18.5 22.3 %collective-permute-start.10 = (f32[8,128]{1,0:T(8,128)}, f32[8,128]{1,0:T(8,128)S(1)}, u32[]{:S(2)}, u32[]{:S(2)}) collective-permute-start(f32[8,128]{1,0:T(8,128)} %get-tuple-element.34), channel_id=1, source_target_pairs={{0,1},{1,0},{2,3},{3,2},{4,5},{5,4},{6,7},{7,6},{8,9},{9,8},{10,11... | collective-permute-start | bytes 12296 | tf_op jit(solution)/shard_map/ppermute | solution.py:24
  22.6 21.6 %copy-start.1 = (bf16[32,2176]{1,0:T(8,128)(2,1)}, bf16[32,2176]{1,0:T(8,128)(2,1)S(1)}, u32[]{:S(2)}) copy-start(bf16[32,2176]{1,0:T(8,128)(2,1)S(1)} %constant_dynamic-update-slice_fusion.refs_0_) | copy-start | bytes 417796
  22.6 7.7 %collective-permute-start.4 = (bf16[32,2176]{1,0:T(8,128)(2,1)S(1)}, bf16[32,2176]{1,0:T(8,128)(2,1)S(1)}, u32[]{:S(2)}, u32[]{:S(2)}) collective-permute-start(bf16[32,2176]{1,0:T(8,128)(2,1)S(1)} %constant_dynamic-update-slice_fusion.refs_0_), channel_id=1, source_target_pairs={{0,2},{1,3},{2,0},{3,1},{4,6},{5,7},{6,4},{7,5},{8,10},{9,11},{10,... | collective-permute-start | bytes 417800 | tf_op jit(solution)/shard_map/ppermute | solution.py:24
  24.2 13.4 %collective-permute-start.6 = (bf16[32,2176]{1,0:T(8,128)(2,1)S(1)}, bf16[32,2176]{1,0:T(8,128)(2,1)S(1)}, u32[]{:S(2)}, u32[]{:S(2)}) collective-permute-start(bf16[32,2176]{1,0:T(8,128)(2,1)S(1)} %constant_dynamic-update-slice_fusion.refs_0_), channel_id=1, source_target_pairs={{0,4},{1,5},{2,6},{3,7},{4,0},{5,1},{6,2},{7,3},{8,12},{9,13},{10,... | collective-permute-start | bytes 417800 | tf_op jit(solution)/shard_map/ppermute | solution.py:24
  26.8 11.4 %collective-permute-start.8 = (bf16[32,2176]{1,0:T(8,128)(2,1)S(1)}, bf16[32,2176]{1,0:T(8,128)(2,1)S(1)}, u32[]{:S(2)}, u32[]{:S(2)}) collective-permute-start(bf16[32,2176]{1,0:T(8,128)(2,1)S(1)} %constant_dynamic-update-slice_fusion.refs_0_), channel_id=1, source_target_pairs={{0,6},{1,7},{2,4},{3,5},{4,2},{5,3},{6,0},{7,1},{8,14},{9,15},{10,... | collective-permute-start | bytes 417800 | tf_op jit(solution)/shard_map/ppermute | solution.py:24
  27.1 15.3 %collective-permute-start.3 = (bf16[32,2176]{1,0:T(8,128)(2,1)S(1)}, bf16[32,2176]{1,0:T(8,128)(2,1)S(1)}, u32[]{:S(2)}, u32[]{:S(2)}) collective-permute-start(bf16[32,2176]{1,0:T(8,128)(2,1)S(1)} %constant_dynamic-update-slice_fusion.refs_0_), channel_id=1, source_target_pairs={{0,1},{1,0},{2,3},{3,2},{4,5},{5,4},{6,7},{7,6},{8,9},{9,8},{10,11... | collective-permute-start | bytes 417800 | tf_op jit(solution)/shard_map/ppermute | solution.py:24
  30.3 13.9 %copy-start.5 = (bf16[32,2176]{1,0:T(8,128)(2,1)}, bf16[32,2176]{1,0:T(8,128)(2,1)S(1)}, u32[]{:S(2)}) copy-start(bf16[32,2176]{1,0:T(8,128)(2,1)S(1)} %collective-permute-done.4.refs_2_) | copy-start | bytes 417796
  30.3 12.1 %collective-permute-start.5 = (bf16[32,2176]{1,0:T(8,128)(2,1)S(1)}, bf16[32,2176]{1,0:T(8,128)(2,1)S(1)}, u32[]{:S(2)}, u32[]{:S(2)}) collective-permute-start(bf16[32,2176]{1,0:T(8,128)(2,1)S(1)} %collective-permute-done.4.refs_2_), channel_id=1, source_target_pairs={{0,1},{1,0},{2,3},{3,2},{4,5},{5,4},{6,7},{7,6},{8,9},{9,8},{10,11... | collective-permute-start | bytes 417800 | tf_op jit(solution)/shard_map/ppermute | solution.py:24
  37.7 6.6 %copy-start.6 = (bf16[32,2176]{1,0:T(8,128)(2,1)}, bf16[32,2176]{1,0:T(8,128)(2,1)S(1)}, u32[]{:S(2)}) copy-start(bf16[32,2176]{1,0:T(8,128)(2,1)S(1)} %collective-permute-done.6.refs_4_) | copy-start | bytes 417796
  37.7 5.1 %collective-permute-start.7 = (bf16[32,2176]{1,0:T(8,128)(2,1)S(1)}, bf16[32,2176]{1,0:T(8,128)(2,1)S(1)}, u32[]{:S(2)}, u32[]{:S(2)}) collective-permute-start(bf16[32,2176]{1,0:T(8,128)(2,1)S(1)} %collective-permute-done.6.refs_4_), channel_id=1, source_target_pairs={{0,1},{1,0},{2,3},{3,2},{4,5},{5,4},{6,7},{7,6},{8,9},{9,8},{10,11... | collective-permute-start | bytes 417800 | tf_op jit(solution)/shard_map/ppermute | solution.py:24
  38.2 6.0 %copy-start.7 = (bf16[32,2176]{1,0:T(8,128)(2,1)}, bf16[32,2176]{1,0:T(8,128)(2,1)S(1)}, u32[]{:S(2)}) copy-start(bf16[32,2176]{1,0:T(8,128)(2,1)S(1)} %collective-permute-done.8.refs_6_) | copy-start | bytes 417796
  38.2 6.0 %collective-permute-start.9 = (bf16[32,2176]{1,0:T(8,128)(2,1)S(1)}, bf16[32,2176]{1,0:T(8,128)(2,1)S(1)}, u32[]{:S(2)}, u32[]{:S(2)}) collective-permute-start(bf16[32,2176]{1,0:T(8,128)(2,1)S(1)} %collective-permute-done.8.refs_6_), channel_id=1, source_target_pairs={{0,1},{1,0},{2,3},{3,2},{4,5},{5,4},{6,7},{7,6},{8,9},{9,8},{10,11... | collective-permute-start | bytes 417800 | tf_op jit(solution)/shard_map/ppermute | solution.py:24
  41.5 30.9 %collective-permute-start.11 = (f32[8,128]{1,0:T(8,128)S(1)}, f32[8,128]{1,0:T(8,128)S(1)}, u32[]{:S(2)}, u32[]{:S(2)}) collective-permute-start(f32[8,128]{1,0:T(8,128)S(1)} %add.89), channel_id=1, source_target_pairs={{0,2},{1,3},{2,0},{3,1},{4,6},{5,7},{6,4},{7,5},{8,10},{9,11},{10,... | collective-permute-start | bytes 12296 | tf_op jit(solution)/shard_map/ppermute | solution.py:24
  42.4 1.8 %copy-start.8 = (bf16[32,2176]{1,0:T(8,128)(2,1)}, bf16[32,2176]{1,0:T(8,128)(2,1)S(1)}, u32[]{:S(2)}) copy-start(bf16[32,2176]{1,0:T(8,128)(2,1)S(1)} %collective-permute-done.3.refs_1_) | copy-start | bytes 417796
  42.4 1.8 %copy-start.9 = (bf16[32,2176]{1,0:T(8,128)(2,1)}, bf16[32,2176]{1,0:T(8,128)(2,1)S(1)}, u32[]{:S(2)}) copy-start(bf16[32,2176]{1,0:T(8,128)(2,1)S(1)} %collective-permute-done.5.refs_3_) | copy-start | bytes 417796
  42.7 1.5 %copy-start.10 = (bf16[32,2176]{1,0:T(8,128)(2,1)}, bf16[32,2176]{1,0:T(8,128)(2,1)S(1)}, u32[]{:S(2)}) copy-start(bf16[32,2176]{1,0:T(8,128)(2,1)S(1)} %collective-permute-done.7.refs_5_) | copy-start | bytes 417796
  44.2 0.7 copy-start.11
  71.8 30.6 %copy-start = (bf16[256,2048]{1,0:T(8,128)(2,1)S(1)}, bf16[256,2048]{1,0:T(8,128)(2,1)}, u32[]{:S(2)}) copy-start(bf16[256,2048]{1,0:T(8,128)(2,1)} %get-tuple-element.48) | copy-start | bytes 3145732
  71.8 9.3 %collective-permute-start.18 = (bf16[48,2048]{1,0:T(8,128)(2,1)}, bf16[48,2048]{1,0:T(8,128)(2,1)S(1)}, u32[]{:S(2)}, u32[]{:S(2)}) collective-permute-start(bf16[48,2048]{1,0:T(8,128)(2,1)} %get-tuple-element.42), channel_id=1, source_target_pairs={{0,1},{1,0},{2,3},{3,2},{4,5},{5,4},{6,7},{7,6},{8,9},{9,8},{10,11... | collective-permute-start | bytes 589832 | tf_op jit(solution)/shard_map/ppermute | solution.py:24
  72.4 4.6 %collective-permute-start.12 = (f32[8,128]{1,0:T(8,128)S(1)}, f32[8,128]{1,0:T(8,128)S(1)}, u32[]{:S(2)}, u32[]{:S(2)}) collective-permute-start(f32[8,128]{1,0:T(8,128)S(1)} %add.90), channel_id=1, source_target_pairs={{0,4},{1,5},{2,6},{3,7},{4,0},{5,1},{6,2},{7,3},{8,12},{9,13},{10,... | collective-permute-start | bytes 12296 | tf_op jit(solution)/shard_map/ppermute | solution.py:24
  77.6 8.0 %collective-permute-start.16 = (bf16[48,2048]{1,0:T(8,128)(2,1)}, bf16[48,2048]{1,0:T(8,128)(2,1)S(1)}, u32[]{:S(2)}, u32[]{:S(2)}) collective-permute-start(bf16[48,2048]{1,0:T(8,128)(2,1)} %get-tuple-element.40), channel_id=1, source_target_pairs={{0,1},{1,0},{2,3},{3,2},{4,5},{5,4},{6,7},{7,6},{8,9},{9,8},{10,11... | collective-permute-start | bytes 589832 | tf_op jit(solution)/shard_map/ppermute | solution.py:24
  79.1 9.4 %collective-permute-start.14 = (bf16[48,2048]{1,0:T(8,128)(2,1)}, bf16[48,2048]{1,0:T(8,128)(2,1)S(1)}, u32[]{:S(2)}, u32[]{:S(2)}) collective-permute-start(bf16[48,2048]{1,0:T(8,128)(2,1)} %get-tuple-element.38), channel_id=1, source_target_pairs={{0,1},{1,0},{2,3},{3,2},{4,5},{5,4},{6,7},{7,6},{8,9},{9,8},{10,11... | collective-permute-start | bytes 589832 | tf_op jit(solution)/shard_map/ppermute | solution.py:24
  79.6 11.0 %collective-permute-start.13 = (bf16[48,2048]{1,0:T(8,128)(2,1)}, bf16[48,2048]{1,0:T(8,128)(2,1)S(1)}, u32[]{:S(2)}, u32[]{:S(2)}) collective-permute-start(bf16[48,2048]{1,0:T(8,128)(2,1)} %get-tuple-element.36), channel_id=1, source_target_pairs={{0,1},{1,0},{2,3},{3,2},{4,5},{5,4},{6,7},{7,6},{8,9},{9,8},{10,11... | collective-permute-start | bytes 589832 | tf_op jit(solution)/shard_map/ppermute | solution.py:24
  82.1 10.2 %collective-permute-start.19 = (bf16[48,2048]{1,0:T(8,128)(2,1)S(1)}, bf16[48,2048]{1,0:T(8,128)(2,1)S(1)}, u32[]{:S(2)}, u32[]{:S(2)}) collective-permute-start(bf16[48,2048]{1,0:T(8,128)(2,1)S(1)} %add_convert_fusion), channel_id=1, source_target_pairs={{0,6},{1,7},{2,4},{3,5},{4,2},{5,3},{6,0},{7,1},{8,14},{9,15},{10,... | collective-permute-start | bytes 589832 | tf_op jit(solution)/shard_map/ppermute | solution.py:24
  86.6 11.8 %collective-permute-start.17 = (bf16[48,2048]{1,0:T(8,128)(2,1)S(1)}, bf16[48,2048]{1,0:T(8,128)(2,1)S(1)}, u32[]{:S(2)}, u32[]{:S(2)}) collective-permute-start(bf16[48,2048]{1,0:T(8,128)(2,1)S(1)} %add_convert_fusion.1), channel_id=1, source_target_pairs={{0,4},{1,5},{2,6},{3,7},{4,0},{5,1},{6,2},{7,3},{8,12},{9,13},{10,... | collective-permute-start | bytes 589832 | tf_op jit(solution)/shard_map/ppermute | solution.py:24
  89.5 9.4 %collective-permute-start.15 = (bf16[48,2048]{1,0:T(8,128)(2,1)S(1)}, bf16[48,2048]{1,0:T(8,128)(2,1)S(1)}, u32[]{:S(2)}, u32[]{:S(2)}) collective-permute-start(bf16[48,2048]{1,0:T(8,128)(2,1)S(1)} %add_convert_fusion.2), channel_id=1, source_target_pairs={{0,2},{1,3},{2,0},{3,1},{4,6},{5,7},{6,4},{7,5},{8,10},{9,11},{10,... | collective-permute-start | bytes 589832 | tf_op jit(solution)/shard_map/ppermute | solution.py:24
  92.3 6.6 %copy-start.2 = (bf16[48,2048]{1,0:T(8,128)(2,1)}, bf16[48,2048]{1,0:T(8,128)(2,1)S(1)}, u32[]{:S(2)}) copy-start(bf16[48,2048]{1,0:T(8,128)(2,1)S(1)} %collective-permute-done.19.refs_3_) | copy-start | bytes 589828
  98.4 0.7 copy-start.3
  98.9 0.7 copy-start.4
  101.8 14.4 %copy-start.14 = (bf16[8,2048]{1,0:T(8,128)(2,1)S(1)}, bf16[8,2048]{1,0:T(8,128)(2,1)}, u32[]{:S(2)}) copy-start(bf16[8,2048]{1,0:T(8,128)(2,1)} %get-tuple-element.43) | copy-start | bytes 98308
  101.8 3.8 %collective-permute-start.23 = (f32[8,128]{1,0:T(8,128)}, f32[8,128]{1,0:T(8,128)S(1)}, u32[]{:S(2)}, u32[]{:S(2)}) collective-permute-start(f32[8,128]{1,0:T(8,128)} %get-tuple-element.47), channel_id=1, source_target_pairs={{0,1},{1,0},{2,3},{3,2},{4,5},{5,4},{6,7},{7,6},{8,9},{9,8},{10,11... | collective-permute-start | bytes 12296 | tf_op jit(solution)/shard_map/ppermute | solution.py:24
  106.3 3.6 %collective-permute-start.24 = (f32[8,128]{1,0:T(8,128)S(1)}, f32[8,128]{1,0:T(8,128)S(1)}, u32[]{:S(2)}, u32[]{:S(2)}) collective-permute-start(f32[8,128]{1,0:T(8,128)S(1)} %add.97), channel_id=1, source_target_pairs={{0,2},{1,3},{2,0},{3,1},{4,6},{5,7},{6,4},{7,5},{8,10},{9,11},{10,... | collective-permute-start | bytes 12296 | tf_op jit(solution)/shard_map/ppermute | solution.py:24
  106.3 9.9 %collective-permute-start.20 = (bf16[8,2048]{1,0:T(8,128)(2,1)}, bf16[8,2048]{1,0:T(8,128)(2,1)S(1)}, u32[]{:S(2)}, u32[]{:S(2)}) collective-permute-start(bf16[8,2048]{1,0:T(8,128)(2,1)} %get-tuple-element.44), channel_id=1, source_target_pairs={{0,8},{8,0},{16,24},{24,16},{1,9},{9,1},{17,25},{25,17},{2,10},{10... | collective-permute-start | bytes 98312 | tf_op jit(solution)/shard_map/ppermute | solution.py:24
  106.3 9.9 %collective-permute-start.21 = (bf16[8,2048]{1,0:T(8,128)(2,1)}, bf16[8,2048]{1,0:T(8,128)(2,1)S(1)}, u32[]{:S(2)}, u32[]{:S(2)}) collective-permute-start(bf16[8,2048]{1,0:T(8,128)(2,1)} %get-tuple-element.45), channel_id=1, source_target_pairs={{0,16},{8,24},{16,0},{24,8},{1,17},{9,25},{17,1},{25,9},{2,18},{10... | collective-permute-start | bytes 98312 | tf_op jit(solution)/shard_map/ppermute | solution.py:24
  107.9 8.3 %collective-permute-start.22 = (bf16[8,2048]{1,0:T(8,128)(2,1)}, bf16[8,2048]{1,0:T(8,128)(2,1)S(1)}, u32[]{:S(2)}, u32[]{:S(2)}) collective-permute-start(bf16[8,2048]{1,0:T(8,128)(2,1)} %get-tuple-element.46), channel_id=1, source_target_pairs={{0,24},{8,16},{16,8},{24,0},{1,25},{9,17},{17,9},{25,1},{2,26},{10... | collective-permute-start | bytes 98312 | tf_op jit(solution)/shard_map/ppermute | solution.py:24
  109.9 4.5 %collective-permute-start.25 = (f32[8,128]{1,0:T(8,128)S(1)}, f32[8,128]{1,0:T(8,128)S(1)}, u32[]{:S(2)}, u32[]{:S(2)}) collective-permute-start(f32[8,128]{1,0:T(8,128)S(1)} %add.98), channel_id=1, source_target_pairs={{0,4},{1,5},{2,6},{3,7},{4,0},{5,1},{6,2},{7,3},{8,12},{9,13},{10,... | collective-permute-start | bytes 12296 | tf_op jit(solution)/shard_map/ppermute | solution.py:24

commit v2 on v0

v2 whole, which is shorter than its diff:
```python
import functools
import jax
import jax.numpy as jnp
from jax import lax
from jax.experimental import pallas as pl
from jax.experimental.pallas import tpu as pltpu
from jax.sharding import PartitionSpec as P

F32 = jnp.float32
BF16 = jnp.bfloat16
LOW = 64
VMEM_SPEC = pl.BlockSpec(memory_space=pltpu.VMEM)
SMEM_SPEC = pl.BlockSpec(memory_space=pltpu.SMEM)
HBM_SPEC = pl.BlockSpec(memory_space=pltpu.HBM)


def split_lat(count):
    inner = 1
    while inner * inner * 4 <= count and count % (inner * 2) == 0:
        inner *= 2
    return count // inner, inner


def shift_to(value, axis, size, mask):
    return lax.ppermute(value, axis, [(i, i ^ mask) for i in range(size)])


def in_vmem(value):
    return pltpu.with_memory_space_constraint(value, pltpu.VMEM)


def in_hbm(value):
    return pltpu.with_memory_space_constraint(value, pltpu.HBM)


def pack_kernel(groups, per_shard, lat_dev, group_ref, res_hbm, slots_hbm, *refs):
    outs, (res_ref, slots_ref, sems) = refs[:groups], refs[groups:]
    copies = [
        pltpu.make_async_copy(slots_hbm, slots_ref, sems.at[0]),
        pltpu.make_async_copy(res_hbm, res_ref, sems.at[1]),
    ]
    for copy in copies:
        copy.start()
    for copy in copies:
        copy.wait()
    group = group_ref[1]
    width = res_ref.shape[2]
    slot_count = slots_ref.shape[2]
    shard = lax.broadcasted_iota(jnp.int32, slots_ref.shape[1:], 1) // per_shard
    for mask in range(groups):
        layer = jnp.bitwise_xor(group, mask)
        slots = slots_ref[layer]
        live = slots >= 0
        local = slots - shard * lat_dev
        high = jnp.where(live, local // LOW, -1)
        low = jnp.where(live, local % LOW, 0)
        outs[mask][:, :width] = res_ref[layer]
        outs[mask][:, width : width + 2 * slot_count] = jnp.concatenate([high, low], axis=1).astype(F32).astype(BF16)


def pack(group, residuals, slots, per_shard, lat_dev):
    groups, rows, width = residuals.shape
    return pl.pallas_call(
        functools.partial(pack_kernel, groups, per_shard, lat_dev),
        out_shape=[pltpu.VMEM((rows, width + 2 * slots.shape[2]), BF16)] * groups,
        in_specs=[SMEM_SPEC, HBM_SPEC, HBM_SPEC],
        out_specs=[VMEM_SPEC] * groups,
        scratch_shapes=[
            pltpu.VMEM(residuals.shape, residuals.dtype),
            pltpu.VMEM(slots.shape, slots.dtype),
            pltpu.SemaphoreType.DMA((2,)),
        ],
        compiler_params=pltpu.CompilerParams(vmem_limit_bytes=4 << 20),
        name="pack",
    )(group, in_hbm(residuals), in_hbm(slots))


def lane_to_line(column):
    eye = lax.broadcasted_iota(jnp.int32, (128, 128), 0) == lax.broadcasted_iota(jnp.int32, (128, 128), 1)
    return jnp.sum(jnp.where(eye, column, 0.0), axis=0, keepdims=True)


def load_kernel(first, rows, tile, after_ref, dict_ref, enc_hbm, dec_hbm, *refs):
    table_ref, lines_ref, total_ref, enc_ref, dec_ref, sems = refs[-6:]
    steps = rows // tile
    small = [
        pltpu.make_async_copy(enc_hbm.at[:, pl.ds(first, rows)], enc_ref, sems.at[steps]),
        pltpu.make_async_copy(dec_hbm, dec_ref, sems.at[steps + 1]),
    ]
    spans = [pl.ds(first + i * tile, tile) for i in range(steps)]
    copies = [pltpu.make_async_copy(dict_ref.at[span], table_ref.at[span], sems.at[i]) for i, span in enumerate(spans)]
    for copy in small + copies:
        copy.start()
    for copy in small:
        copy.wait()
    total = jnp.zeros((1, 1), F32) if first == 0 else refs[2][0:1, 0:1]
    for i in range(steps):
        copies[i].wait()
        for start in range(i * tile, (i + 1) * tile, 128):
            span = slice(first + start, first + start + 128)
            values = table_ref[span].astype(F32)
            norm = jnp.sqrt(lane_to_line(jnp.sum(values * values, axis=1, keepdims=True)) + 1e-06)
            shift = lane_to_line(jnp.sum(values * dec_ref[...], axis=1, keepdims=True))
            inverse = 1.0 / norm
            lines_ref[0:1, span] = inverse
            lines_ref[1:2, span] = enc_ref[:, start : start + 128] - shift * inverse
            total += jnp.sum(norm, keepdims=True)
    total_ref[...] = jnp.broadcast_to(total, total_ref.shape)


def load(before, after, dictionary, enc_bias, dec_bias, first, rows, tile):
    lat_dev, width = dictionary.shape
    return pl.pallas_call(
        functools.partial(load_kernel, first, rows, tile),
        out_shape=[
            pltpu.VMEM((lat_dev, width), BF16),
            pltpu.VMEM((2, lat_dev), F32),
            pltpu.VMEM((8, 128), F32),
        ],
        in_specs=[VMEM_SPEC, HBM_SPEC, HBM_SPEC, HBM_SPEC] + [VMEM_SPEC] * len(before),
        out_specs=[VMEM_SPEC] * 3,
        scratch_shapes=[
            pltpu.VMEM((1, rows), F32),
            pltpu.VMEM((1, width), F32),
            pltpu.SemaphoreType.DMA((rows // tile + 2,)),
        ],
        input_output_aliases={4 + i: i for i in range(len(before))},
        compiler_params=pltpu.CompilerParams(vmem_limit_bytes=24 << 20),
        name="load",
    )(
        in_vmem(after),
        in_hbm(dictionary),
        in_hbm(enc_bias),
        in_hbm(dec_bias),
        *[in_vmem(value) for value in before],
    )


def main_kernel(
    parts, blocks, outer, chunk, tok_dev, per_shard, slot_count, r_dev, tile, span, place_ref, seed_ref, *refs
):
    tables, refs = refs[:parts], refs[parts:]
    lines, refs = refs[:parts], refs[parts:]
    norm_parts, refs = refs[:parts], refs[parts:]
    ins, refs = refs[:blocks], refs[blocks:]
    shares, refs = refs[:blocks], refs[blocks:]
    inner = blocks // outer
    seed_shares, refs = refs[:inner], refs[inner:]
    normed, seed_features, norm_total, mass_ref, ids, weights, product, coefficients, chosen_rows = refs
    shard, group = place_ref[0], place_ref[1]
    part_rows, width = tables[0].shape
    rows = ins[0].shape[0]
    tokens = rows * blocks
    now = rows * chunk

    norm_total[...] = sum(part[...] for part in norm_parts)
    total = jnp.zeros((1, 1), F32)
    for block in ins:
        raw = block[:, :width].astype(F32)
        total += jnp.sum(raw * raw, keepdims=True)
    scale = lax.rsqrt(total / (tokens * width))
    for k, block in enumerate(ins):
        normed[k * rows : (k + 1) * rows, :] = (block[:, :width].astype(F32) * scale).astype(BF16)

    shape = (2 * slot_count, per_shard * 128)
    source = lax.broadcasted_iota(jnp.int32, shape, 0)
    wanted = lax.broadcasted_iota(jnp.int32, shape, 1) // 128 + shard * per_shard
    chooser = jnp.where(source == wanted, float(LOW), jnp.where(source == wanted + slot_count, 1.0, 0.0)).astype(BF16)
    lanes = [slice(c * 128, (c + 1) * 128) for c in range(per_shard)]
    lane = lax.broadcasted_iota(jnp.int32, (1, 128), 1)
    seeds = seed_ref[...]
    unit = seeds // tok_dev
    places = (
        jnp.bitwise_xor(unit % blocks, shard) * rows
        + jnp.bitwise_xor(unit // blocks, group) * tok_dev
        + seeds % tok_dev
    )
    rows_for = lambda k: pl.ds(pl.multiple_of(jnp.bitwise_xor(shard, k) * r_dev, r_dev), r_dev)
    place = lax.broadcasted_iota(jnp.int32, (tokens, r_dev * blocks), 0)
    chosen = jnp.where(place == places, 1.0, 0.0).astype(BF16)

    def pick(which, values):
        return lax.dot_general(which, values, (((0,), (0,)), ((), ())), preferred_element_type=F32).astype(BF16)

    chosen_rows[...] = pick(chosen, normed[...])
    seed_features[...] = chosen_rows[rows_for(0)]

    for lead in range(0, blocks, chunk):
        members = slice(lead * rows, lead * rows + now)
        coded = jnp.concatenate([block[:, width:] for block in ins[lead : lead + chunk]], axis=0)
        ids[...] = jnp.dot(coded, chooser, preferred_element_type=F32)
        for c in range(per_shard):
            weights[:, lanes[c]] = sum(jnp.where(ids[:, lanes[c]] == ids[:, other], 1.0, 0.0) for other in lanes)
        for part in range(parts):
            for first in range(0, part_rows, tile):
                product[...] = lax.dot_general(
                    normed[members],
                    tables[part][first : first + tile],
                    (((1,), (1,)), ((), ())),
                    preferred_element_type=F32,
                )
                for j in range(0, tile, 128):
                    local = slice(first + j, first + j + 128)
                    columns = slice(part * part_rows + first + j, part * part_rows + first + j + 128)
                    latent = (lane + columns.start).astype(F32)
                    inverse = lines[part][0:1, local]
                    offset = lines[part][1:2, local]
                    count = jnp.zeros((now, 128), F32)
                    for c in range(per_shard):
                        count = jnp.where(ids[:, lanes[c]] == latent, weights[:, lanes[c]], count)
                    activity = jnp.maximum(product[:, j : j + 128] * inverse + offset, 0.0)
                    mass = jnp.sum(activity * count, axis=0, keepdims=True)
                    mass_ref[:, columns] = mass if lead == 0 else mass_ref[:, columns] + mass
                    coefficients[:, columns] = (activity * inverse).astype(BF16) * count.astype(BF16)
        for start in range(0, width, span):
            columns = slice(start, start + span)
            share = sum(
                jnp.dot(
                    coefficients[:, part * part_rows : (part + 1) * part_rows],
                    tables[part][:, columns],
                    preferred_element_type=F32,
                )
                for part in range(parts)
            ).astype(BF16)
            picked = pick(chosen[members], share)
            chosen_rows[:, columns] = picked if lead == 0 else chosen_rows[:, columns] + picked
            for k in range(chunk):
                shares[lead + k][:, columns] = share[k * rows : (k + 1) * rows]
    for k in range(blocks):
        z, x = k // inner, k % inner
        seed_shares[x][z * r_dev : (z + 1) * r_dev] = chosen_rows[rows_for(k)]


def main(place, seeds, loaded, blocks, outer, tok_dev, per_shard, slot_count, tile, span):
    tables, lines, norm_parts = [[value] for value in loaded]
    part_rows, width = tables[0].shape
    parts = len(tables)
    lat_dev = part_rows * parts
    count = len(blocks)
    rows = blocks[0].shape[0]
    tokens = rows * count
    chunk = max(1, min(count, 512 // rows))
    now = chunk * rows
    r_dev = seeds.shape[1] // count
    arrays = [in_vmem(value) for value in (*tables, *lines, *norm_parts, *blocks)]
    results = pl.pallas_call(
        functools.partial(
            main_kernel, parts, count, outer, chunk, tok_dev, per_shard, slot_count, r_dev, tile, span
        ),
        out_shape=[pltpu.VMEM((rows, width), BF16)] * count
        + [pltpu.VMEM((outer * r_dev, width), BF16)] * (count // outer)
        + [
            pltpu.VMEM((tokens, width), BF16),
            pltpu.VMEM((r_dev, width), BF16),
            pltpu.VMEM((8, 128), F32),
            jax.ShapeDtypeStruct((1, lat_dev), F32),
        ],
        in_specs=[SMEM_SPEC, VMEM_SPEC] + [VMEM_SPEC] * len(arrays),
        out_specs=[VMEM_SPEC] * (count + count // outer + 4),
        scratch_shapes=[
            pltpu.VMEM((now, per_shard * 128), F32),
            pltpu.VMEM((now, per_shard * 128), F32),
            pltpu.VMEM((now, tile), F32),
            pltpu.VMEM((now, lat_dev), BF16),
            pltpu.VMEM((r_dev * count, width), BF16),
        ],
        compiler_params=pltpu.CompilerParams(vmem_limit_bytes=24 << 20),
        name="sparse_code",
    )(place, seeds, *arrays)
    return results[:count], results[count:-4], results[-4:]


def token_kernel(parts, groups, normed_ref, dec_ref, norm_ref, *refs):
    shares, refs = refs[:parts], refs[parts:]
    *recon, stats_ref = refs
    summed = shares[0][...].astype(F32)
    for share in shares[1:]:
        summed += share[...].astype(F32)
    estimate = summed + dec_ref[...]
    rows = estimate.shape[0]
    size = rows // groups
    for k in range(groups):
        recon[k][...] = estimate[k * size : (k + 1) * size].astype(BF16)
    errors = normed_ref[:rows].astype(F32) - estimate
    line = lax.broadcasted_iota(jnp.int32, stats_ref.shape, 0)
    stats_ref[...] = jnp.where(line == 0, jnp.sum(errors * errors, keepdims=True), norm_ref[...])


def finish_tokens(shares, normed, dec_bias, norm_part, groups):
    rows, width = shares[0].shape
    return pl.pallas_call(
        functools.partial(token_kernel, len(shares), groups),
        out_shape=[pltpu.VMEM((rows // groups, width), BF16)] * groups + [pltpu.VMEM((8, 128), F32)],
        in_specs=[VMEM_SPEC] * (3 + len(shares)),
        out_specs=[VMEM_SPEC] * (groups + 1),
        compiler_params=pltpu.CompilerParams(vmem_limit_bytes=8 << 20),
        name="finish_tokens",
    )(in_vmem(normed), dec_bias, in_vmem(norm_part), *[in_vmem(share) for share in shares])


def seed_sum_kernel(inner, *refs):
    shares, refs = refs[:inner], refs[inner:]
    stats, refs = refs[:inner], refs[inner:]
    mine_ref, stats_ref, *outs = refs
    r_dev, width = mine_ref.shape
    total = sum(stat[...] for stat in stats)
    stats_ref[...] = total
    line = jnp.zeros((1, 128), F32)
    lane = lax.broadcasted_iota(jnp.int32, (1, 128), 1)
    for which in range(2):
        rest = total[which : which + 1]
        for part in range(3):
            piece = rest.astype(BF16).astype(F32)
            line = jnp.where(lane == which * 3 + part, piece, line)
            rest = rest - piece
    line = jnp.broadcast_to(line, (r_dev, 128)).astype(BF16)
    for z, out in enumerate([mine_ref, *outs]):
        span = slice(z * r_dev, (z + 1) * r_dev)
        out[:, :width] = sum(share[span].astype(F32) for share in shares).astype(out.dtype)
        if z:
            out[:, width:] = line


def sum_seeds(shares, stats, outer):
    rows, width = shares[0].shape
    rows //= outer
    return pl.pallas_call(
        functools.partial(seed_sum_kernel, len(shares)),
        out_shape=[pltpu.VMEM((rows, width), F32), pltpu.VMEM((8, 128), F32)]
        + [pltpu.VMEM((rows, width + 128), BF16)] * (outer - 1),
        in_specs=[VMEM_SPEC] * (len(shares) + len(stats)),
        out_specs=[VMEM_SPEC] * (outer + 1),
        compiler_params=pltpu.CompilerParams(vmem_limit_bytes=8 << 20),
        name="sum_seeds",
    )(*[in_vmem(value) for value in (*shares, *stats)])


def seed_kernel(latents, features_ref, dec_ref, spread_ref, mine_ref, stats_ref, *refs):
    *shares, rows_ref, unexplained_ref = refs
    width = mine_ref.shape[1]
    summed = mine_ref[...]
    line = jnp.zeros((1, 128), F32)
    for share in shares:
        summed += share[:, :width].astype(F32)
        line += share[0:1, width:].astype(F32)
    lane = lax.broadcasted_iota(jnp.int32, (1, 128), 1)
    numerator = stats_ref[0:1, 0:1] + jnp.sum(jnp.where(lane < 3, line, 0.0), keepdims=True)
    norm_sum = stats_ref[1:2, 0:1] + jnp.sum(jnp.where((lane >= 3) & (lane < 6), line, 0.0), keepdims=True)
    seeds = features_ref[...].astype(F32) - (summed + dec_ref[...])
    norm = jnp.sqrt(jnp.sum(seeds * seeds, axis=1, keepdims=True) + 1e-06)
    rows_ref[...] = (seeds / norm * (norm_sum / latents)).astype(BF16)
    unexplained_ref[...] = numerator / spread_ref[...]


def finish_seeds(shares, features, dec_bias, spread, latents):
    return pl.pallas_call(
        functools.partial(seed_kernel, latents),
        out_shape=[jax.ShapeDtypeStruct(features.shape, BF16), jax.ShapeDtypeStruct((1, 1), F32)],
        in_specs=[VMEM_SPEC] * (3 + len(shares)),
        out_specs=[VMEM_SPEC] * 2,
        compiler_params=pltpu.CompilerParams(vmem_limit_bytes=8 << 20),
        name="finish_seeds",
    )(in_vmem(features), dec_bias, in_vmem(spread), *[in_vmem(value) for value in shares])


def side_kernel(chunk, place_ref, normed_ref, dead_ref, enc_ref, spread_ref, bias_ref):
    tokens, width = normed_ref.shape
    lat_dev = enc_ref.shape[1]
    total = jnp.zeros((1, 1), F32)
    for start in range(0, width, chunk):
        values = normed_ref[:, start : start + chunk].astype(F32)
        centered = values - jnp.sum(values, axis=0, keepdims=True) / tokens
        total += jnp.sum(centered * centered, keepdims=True)
    spread_ref[...] = total
    latent = lax.broadcasted_iota(jnp.int32, (1, lat_dev), 1) + place_ref[0] * lat_dev
    eye = lax.broadcasted_iota(jnp.int32, (128, 128), 0) == lax.broadcasted_iota(jnp.int32, (128, 128), 1)
    hits = jnp.zeros((1, lat_dev), jnp.int32)
    for start in range(0, dead_ref.shape[1], 128):
        dead = jnp.sum(jnp.where(eye, dead_ref[:, start : start + 128], 0), axis=1, keepdims=True)
        hits = jnp.maximum(hits, jnp.max(jnp.where(dead == latent, 1, 0), axis=0, keepdims=True))
    bias_ref[...] = jnp.where(hits > 0, 0.0, enc_ref[...])


def side(place, normed, dead_ids, enc_bias):
    return pl.pallas_call(
        functools.partial(side_kernel, 256),
        out_shape=[pltpu.VMEM((1, 1), F32), jax.ShapeDtypeStruct(enc_bias.shape, F32)],
        in_specs=[SMEM_SPEC] + [VMEM_SPEC] * 3,
        out_specs=[VMEM_SPEC] * 2,
        compiler_params=pltpu.CompilerParams(vmem_limit_bytes=8 << 20),
        name="side",
    )(place, in_vmem(normed), dead_ids, enc_bias)


def unpack_kernel(group_ref, *refs):
    *parts, out_ref = refs
    for mask, part in enumerate(parts):
        out_ref[jnp.bitwise_xor(group_ref[1], mask)] = part[...]


def unpack(group, parts):
    return pl.pallas_call(
        unpack_kernel,
        out_shape=jax.ShapeDtypeStruct((len(parts), *parts[0].shape), BF16),
        in_specs=[SMEM_SPEC] + [VMEM_SPEC] * len(parts),
        out_specs=VMEM_SPEC,
        compiler_params=pltpu.CompilerParams(vmem_limit_bytes=4 << 20),
        name="unpack",
    )(group, *[in_vmem(part) for part in parts])


LOADS = 4


def body(residuals, topk_slots, dictionary, enc_bias, dec_bias, dead_ids, seed_tokens):
    tok_dev = residuals.shape[1]
    lat_count = lax.axis_size("lat")
    groups = lax.axis_size("layer")
    shard = lax.axis_index("lat")
    group = lax.axis_index("layer")
    lat_dev = dictionary.shape[1]
    slot_count = topk_slots.shape[2]
    per_shard = slot_count // lat_count
    outer, inner = split_lat(lat_count)
    lat = lambda value, mask: shift_to(value, "lat", lat_count, mask)
    layer = lambda value, mask: shift_to(value, "layer", groups, mask)
    place = jnp.stack([shard, group])

    packed = pack(place, residuals, topk_slots, per_shard, lat_dev)
    mine = jnp.concatenate([packed[0]] + [layer(packed[k], k) for k in range(1, groups)], axis=0)
    columns = [mine] + [lat(mine, inner * z) for z in range(1, outer)]
    blocks = [block for column in columns for block in [column] + [lat(column, x) for x in range(1, inner)]]

    part_rows = lat_dev // LOADS
    loaded = ()
    for part, after in enumerate((packed[0], mine, columns[-1], columns[-1])):
        loaded = load(loaded, after, dictionary[0], enc_bias, dec_bias, part * part_rows, part_rows, part_rows // 4)
    shares, seed_shares, (normed, seed_features, norm_part, mass) = main(
        place, seed_tokens, loaded, blocks, outer, tok_dev, per_shard, slot_count, 1024, 1024
    )

    sums = [None] * outer
    for z in reversed(range(outer)):
        total = shares[z * inner].astype(F32)
        for x in range(1, inner):
            total = total + lat(shares[z * inner + x], x).astype(F32)
        sums[z] = total
    last = [sums[0]] + [lat(sums[z].astype(BF16), inner * z) for z in range(1, outer)]
    spread, new_bias = side(place, normed, dead_ids, enc_bias)
    *recon, stats = finish_tokens(last, normed, dec_bias, norm_part, groups)
    reconstruction = unpack(place, [recon[0]] + [layer(recon[k], k) for k in range(1, groups)])
    seed_sums = sum_seeds(
        [seed_shares[0]] + [lat(seed_shares[x], x) for x in range(1, inner)],
        [stats] + [lat(stats, x) for x in range(1, inner)],
        outer,
    )
    seed_last = list(seed_sums[:2]) + [lat(seed_sums[z + 1], inner * z) for z in range(1, outer)]
    new_rows, unexplained = finish_seeds(seed_last, seed_features, dec_bias, spread, lat_dev * lat_count)
    return (reconstruction, unexplained.reshape(1), mass, new_rows[None], new_bias)


def solution(mesh):
    in_specs = (
        P(None, ("layer", "lat"), None),
        P(None, ("layer", "lat"), None),
        P("layer", "lat", None),
        P("layer", "lat"),
        P("layer", None),
        P("layer", None),
        P("layer", None),
    )
    out_specs = (
        P(None, ("layer", "lat"), None),
        P("layer"),
        P("layer", "lat"),
        P("layer", "lat", None),
        P("layer", "lat"),
    )
    return jax.shard_map(body, mesh=mesh, in_specs=in_specs, out_specs=out_specs, check_vma=False)
```

time: 292 us -> 86.5 us (0.30)
  local copies, waits for them, and re-layouts: 69 us -> 0.06 us
  waiting for transfers between devices: 73.1 us -> 24.1 us
  blocking collectives: 41.5 us -> 0 us
  other arithmetic: 41.2 us -> 0.2 us
  matrix products: 32.6 us -> 0 us
  Pallas kernels: 0 us -> 32.6 us
  between operations: 17.4 us -> 0.82 us
  starting transfers between devices: 16.5 us -> 28.5 us
    psum x1 -> x0, waiting for transfers between devices: 62.3 us -> none  [body(): lax.psum(partial_value.astype(jnp.bfloat16), 'lat').astype(jnp.float32)]
    gather x8 -> x0, local copies, waits for them, and re-layouts: 60.4 us -> none  [the longest x1 24.4 us: body(): picked = jnp.take(shard_rows, clipped, axis=0)]
    psum x1 -> x0, blocking collectives: 41.5 us -> none  [body(): totals, norm_totals = lax.psum((squares, norm_vector), ('layer', 'lat'))]
    dot_general x3 -> x0, matrix products: 32.6 us -> none  [the longest x1 13 us: body(): jnp.dot(shard_rows, dec_bias[0], precision=lax.Precision.HIGHEST, preferr...]
    pallas_call x0 -> x11, Pallas kernels: none -> 32.6 us  [the longest x1 13.4 us: main(): pl.pallas_call(functools.partial(main_kernel, parts, count, outer, chunk,...]
    ppermute x0 -> x25, starting transfers between devices: none -> 28.5 us  [shift_to(): return lax.ppermute(value, axis, [(i, i ^ mask) for i in range(size)])]
    ppermute x0 -> x25, waiting for transfers between devices: none -> 24.1 us  [shift_to(): return lax.ppermute(value, axis, [(i, i ^ mask) for i in range(size)])]
    all_to_all x4 -> x0, starting transfers between devices: 16.2 us -> none  [the longest x1 5.31 us: body(): lax.all_to_all(lax.all_to_all(topk_slots, 'layer', split_axis=0, concat_a...]
  transfers between devices with their start and end apart: 6 -> 25, of which waited for: 4 -> 14; matrix products, arithmetic and copies ran while one was open for 37% -> 0% of each run, Pallas kernels for 0% -> 19%
where the time goes in v2:
time: 86.5 us; the launch traced here: 86.2 us
  Pallas kernels  32.6 us (38%)
  starting transfers between devices  28.5 us (33%)
  waiting for transfers between devices  24.1 us (28%)
    ppermute x25, starting transfers between devices, shift_to(): return lax.ppermute(value, axis, [(i, i ^ mask) for i in range(size)])  28.5 us
    ppermute x25, waiting for transfers between devices, shift_to(): return lax.ppermute(value, axis, [(i, i ^ mask) for i in range(size)])  24.1 us
    pallas_call x1, Pallas kernels, main(): pl.pallas_call(functools.partial(main_kernel, parts, count, outer, chunk,...  13.4 us
    pallas_call x4, Pallas kernels, load(): pl.pallas_call(functools.partial(load_kernel, first, rows, tile), out_sha...  12.6 us
    pallas_call x1, Pallas kernels, side(): pl.pallas_call(functools.partial(side_kernel, 256), out_shape=[pltpu.VMEM...  2.08 us
  transfers between devices with their start and end apart: 25, of which 14 were waited for; matrix products, arithmetic and copies ran while one was open for 0% of the time, Pallas kernels for 19%

profile of v2, /device:TPU:0, one launch (start us, length us, event | category | flops | bytes accessed | tf_op | source)
XLA Modules:
  0.0 86.2 jit_solution(10245877093339278108)
XLA Ops:
  0.6 0.1 pad_add_fusion.group_ref.place_ref
  0.7 1.6 %pack.1 = (bf16[8,2176]{1,0:T(8,128)(2,1)S(1)}, bf16[8,2176]{1,0:T(8,128)(2,1)S(1)}, bf16[8,2176]{1,0:T(8,128)(2,1)S(1)}, bf16[8,2176]{1,0:T(8,128)(2,1)S(1)}) custom-call(s32[2]{0:T(128)S(1)} %pad_add_fusion.group_ref.place_ref, bf16[4,8,2048]{2,1,0:T(8,128)(2,1)} %res_hbm.1, s32[4,8,64]{2,1,0:T(8,128)} %slots_hbm.1), custom_call_target="tpu_custom_call" | custom-call | tf_op jit(solution)/shard_map/pack/pallas_call | solution.py:63
  2.3 0.6 collective-permute-start
  2.9 2.6 %collective-permute-start.1 = (bf16[8,2176]{1,0:T(8,128)(2,1)S(1)}, bf16[8,2176]{1,0:T(8,128)(2,1)S(1)}, u32[]{:S(2)}, u32[]{:S(2)}) collective-permute-start(bf16[8,2176]{1,0:T(8,128)(2,1)S(1)} %get-tuple-element.51), channel_id=1, source_target_pairs={{0,16},{8,24},{16,0},{24,8},{1,17},{9,25},{17,1},{25,9},{2,18},{10... | collective-permute-start | bytes 104456 | tf_op jit(solution)/shard_map/ppermute | solution.py:25
  5.4 0.0 collective-permute-start.2
  5.5 0.0 collective-permute-done
  5.5 2.0 %collective-permute-done.1 = bf16[8,2176]{1,0:T(8,128)(2,1)S(1)} collective-permute-done((bf16[8,2176]{1,0:T(8,128)(2,1)S(1)}, bf16[8,2176]{1,0:T(8,128)(2,1)S(1)}, u32[]{:S(2)}, u32[]{:S(2)}) %collective-permute-start.1) | collective-permute-done | bytes 34848 | tf_op jit(solution)/shard_map/ppermute | solution.py:25
  7.5 1.4 %collective-permute-done.2 = bf16[8,2176]{1,0:T(8,128)(2,1)S(1)} collective-permute-done((bf16[8,2176]{1,0:T(8,128)(2,1)S(1)}, bf16[8,2176]{1,0:T(8,128)(2,1)S(1)}, u32[]{:S(2)}, u32[]{:S(2)}) %collective-permute-start.2) | collective-permute-done | bytes 34848 | tf_op jit(solution)/shard_map/ppermute | solution.py:25
  8.8 3.6 %collective-permute-start.3 = (bf16[32,2176]{1,0:T(8,128)(2,1)S(1)}, bf16[32,2176]{1,0:T(8,128)(2,1)S(1)}, u32[]{:S(2)}, u32[]{:S(2)}) collective-permute-start(bf16[32,2176]{1,0:T(8,128)(2,1)S(1)} %constant_dynamic-update-slice_fusion.after_ref.refs_3_), channel_id=1, source_target_pairs={{0,6},{1,7},{2,4},{3,5},{4,2},{5,3},{6,0},{7,1},{8,14},{9,15},{10,... | collective-permute-start | bytes 417800 | tf_op jit(solution)/shard_map/ppermute | solution.py:25
  12.4 0.0 collective-permute-start.5
  12.4 0.8 collective-permute-start.7
  13.2 1.5 %collective-permute-start.4 = (bf16[32,2176]{1,0:T(8,128)(2,1)S(1)}, bf16[32,2176]{1,0:T(8,128)(2,1)S(1)}, u32[]{:S(2)}, u32[]{:S(2)}) collective-permute-start(bf16[32,2176]{1,0:T(8,128)(2,1)S(1)} %constant_dynamic-update-slice_fusion.after_ref.refs_3_), channel_id=1, source_target_pairs={{0,1},{1,0},{2,3},{3,2},{4,5},{5,4},{6,7},{7,6},{8,9},{9,8},{10,11... | collective-permute-start | bytes 417800 | tf_op jit(solution)/shard_map/ppermute | solution.py:25
  14.7 2.5 %collective-permute-done.3.after_ref.refs_9_ = bf16[32,2176]{1,0:T(8,128)(2,1)S(1)} collective-permute-done((bf16[32,2176]{1,0:T(8,128)(2,1)S(1)}, bf16[32,2176]{1,0:T(8,128)(2,1)S(1)}, u32[]{:S(2)}, u32[]{:S(2)}) %collective-permute-start.3) | collective-permute-done | bytes 139296 | tf_op jit(solution)/shard_map/ppermute | solution.py:25
  17.2 1.5 %collective-permute-start.9 = (bf16[32,2176]{1,0:T(8,128)(2,1)S(1)}, bf16[32,2176]{1,0:T(8,128)(2,1)S(1)}, u32[]{:S(2)}, u32[]{:S(2)}) collective-permute-start(bf16[32,2176]{1,0:T(8,128)(2,1)S(1)} %collective-permute-done.3.after_ref.refs_9_), channel_id=1, source_target_pairs={{0,1},{1,0},{2,3},{3,2},{4,5},{5,4},{6,7},{7,6},{8,9},{9,8},{10,11... | collective-permute-start | bytes 417800 | tf_op jit(solution)/shard_map/ppermute | solution.py:25
  18.7 1.8 %collective-permute-done.5.refs_5_ = bf16[32,2176]{1,0:T(8,128)(2,1)S(1)} collective-permute-done((bf16[32,2176]{1,0:T(8,128)(2,1)S(1)}, bf16[32,2176]{1,0:T(8,128)(2,1)S(1)}, u32[]{:S(2)}, u32[]{:S(2)}) %collective-permute-start.5) | collective-permute-done | bytes 139296 | tf_op jit(solution)/shard_map/ppermute | solution.py:25
  20.5 1.5 %collective-permute-start.6 = (bf16[32,2176]{1,0:T(8,128)(2,1)S(1)}, bf16[32,2176]{1,0:T(8,128)(2,1)S(1)}, u32[]{:S(2)}, u32[]{:S(2)}) collective-permute-start(bf16[32,2176]{1,0:T(8,128)(2,1)S(1)} %collective-permute-done.5.refs_5_), channel_id=1, source_target_pairs={{0,1},{1,0},{2,3},{3,2},{4,5},{5,4},{6,7},{7,6},{8,9},{9,8},{10,11... | collective-permute-start | bytes 417800 | tf_op jit(solution)/shard_map/ppermute | solution.py:25
  22.0 2.5 %collective-permute-done.7.refs_7_ = bf16[32,2176]{1,0:T(8,128)(2,1)S(1)} collective-permute-done((bf16[32,2176]{1,0:T(8,128)(2,1)S(1)}, bf16[32,2176]{1,0:T(8,128)(2,1)S(1)}, u32[]{:S(2)}, u32[]{:S(2)}) %collective-permute-start.7) | collective-permute-done | bytes 139296 | tf_op jit(solution)/shard_map/ppermute | solution.py:25
  24.5 1.5 %collective-permute-start.8 = (bf16[32,2176]{1,0:T(8,128)(2,1)S(1)}, bf16[32,2176]{1,0:T(8,128)(2,1)S(1)}, u32[]{:S(2)}, u32[]{:S(2)}) collective-permute-start(bf16[32,2176]{1,0:T(8,128)(2,1)S(1)} %collective-permute-done.7.refs_7_), channel_id=1, source_target_pairs={{0,1},{1,0},{2,3},{3,2},{4,5},{5,4},{6,7},{7,6},{8,9},{9,8},{10,11... | collective-permute-start | bytes 417800 | tf_op jit(solution)/shard_map/ppermute | solution.py:25
  26.0 3.1 %load.4 = (bf16[4096,2048]{1,0:T(8,128)(2,1)S(1)}, f32[2,4096]{1,0:T(2,128)S(1)}, f32[8,128]{1,0:T(8,128)S(1)}) custom-call(bf16[8,2176]{1,0:T(8,128)(2,1)S(1)} %get-tuple-element.49.after_ref, bf16[4096,2048]{1,0:T(8,128)(2,1)} %bitcast.5, f32[1,4096]{1,0:T(1,128)} %enc_ref.1, f32[1,2048]{1,0:T(1,128)} %dec_ref.3), custom_call_target="tpu_custom_call" | custom-call | tf_op jit(solution)/shard_map/load/pallas_call | solution.py:113
  29.2 3.1 %load.5 = (bf16[4096,2048]{1,0:T(8,128)(2,1)S(1)}, f32[2,4096]{1,0:T(2,128)S(1)}, f32[8,128]{1,0:T(8,128)S(1)}) custom-call(bf16[32,2176]{1,0:T(8,128)(2,1)S(1)} %constant_dynamic-update-slice_fusion.after_ref.refs_3_, bf16[4096,2048]{1,0:T(8,128)(2,1)} %bitcast.6, f32[1,4096]{1,0:T(1,128)} %enc_ref.1, ...), custom_call_target="tpu_custom_call", output_to_operand_aliasing={{0}: (4, {}), {1}: (5, {}), {2}: (6, {})} | custom-call | tf_op jit(solution)/shard_map/load/pallas_call | solution.py:113
  32.3 3.1 %load.6 = (bf16[4096,2048]{1,0:T(8,128)(2,1)S(1)}, f32[2,4096]{1,0:T(2,128)S(1)}, f32[8,128]{1,0:T(8,128)S(1)}) custom-call(bf16[32,2176]{1,0:T(8,128)(2,1)S(1)} %collective-permute-done.3.after_ref.refs_9_, bf16[4096,2048]{1,0:T(8,128)(2,1)} %bitcast.7, f32[1,4096]{1,0:T(1,128)} %enc_ref.1, ...), custom_call_target="tpu_custom_call", output_to_operand_aliasing={{0}: (4, {}), {1}: (5, {}), {2}: (6, {})} | custom-call | tf_op jit(solution)/shard_map/load/pallas_call | solution.py:113
  35.5 0.0 copy-start.2
  35.5 3.1 %load.7 = (bf16[4096,2048]{1,0:T(8,128)(2,1)S(1)}, f32[2,4096]{1,0:T(2,128)S(1)}, f32[8,128]{1,0:T(8,128)S(1)}) custom-call(bf16[32,2176]{1,0:T(8,128)(2,1)S(1)} %collective-permute-done.3.after_ref.refs_9_, bf16[4096,2048]{1,0:T(8,128)(2,1)} %bitcast.8, f32[1,4096]{1,0:T(1,128)} %enc_ref.1, ...), custom_call_target="tpu_custom_call", output_to_operand_aliasing={{0}: (4, {}), {1}: (5, {}), {2}: (6, {})} | custom-call | tf_op jit(solution)/shard_map/load/pallas_call | solution.py:113
  38.6 0.0 copy-start.1
  38.7 0.0 copy-start
  38.7 0.0 copy-start.3
  38.7 0.0 collective-permute-done.4.refs_4_
  38.7 0.0 collective-permute-done.9.refs_10_
  38.7 0.0 collective-permute-done.6.refs_6_
  38.7 0.0 collective-permute-done.8.refs_8_
  38.7 13.4 %sparse_code.1 = (bf16[32,2048]{1,0:T(8,128)(2,1)S(1)}, bf16[32,2048]{1,0:T(8,128)(2,1)S(1)}, bf16[32,2048]{1,0:T(8,128)(2,1)S(1)}, bf16[32,2048]{1,0:T(8,128)(2...) custom-call(s32[2]{0:T(128)S(1)} %pad_add_fusion.group_ref.place_ref, ...), custom_call_target="tpu_custom_call" | custom-call | tf_op jit(solution)/shard_map/sparse_code/pallas_call | solution.py:246
  52.1 0.5 collective-permute-start.15
  52.7 1.5 %collective-permute-start.13 = (bf16[32,2048]{1,0:T(8,128)(2,1)S(1)}, bf16[32,2048]{1,0:T(8,128)(2,1)S(1)}, u32[]{:S(2)}, u32[]{:S(2)}) collective-permute-start(bf16[32,2048]{1,0:T(8,128)(2,1)S(1)} %get-tuple-element.72), channel_id=1, source_target_pairs={{0,1},{1,0},{2,3},{3,2},{4,5},{5,4},{6,7},{7,6},{8,9},{9,8},{10,11... | collective-permute-start | bytes 393224 | tf_op jit(solution)/shard_map/ppermute | solution.py:25
  54.2 0.5 collective-permute-start.11
  54.7 1.5 %collective-permute-start.10 = (bf16[32,2048]{1,0:T(8,128)(2,1)S(1)}, bf16[32,2048]{1,0:T(8,128)(2,1)S(1)}, u32[]{:S(2)}, u32[]{:S(2)}) collective-permute-start(bf16[32,2048]{1,0:T(8,128)(2,1)S(1)} %get-tuple-element.68), channel_id=1, source_target_pairs={{0,1},{1,0},{2,3},{3,2},{4,5},{5,4},{6,7},{7,6},{8,9},{9,8},{10,11... | collective-permute-start | bytes 393224 | tf_op jit(solution)/shard_map/ppermute | solution.py:25
  56.2 0.5 collective-permute-start.20
  56.7 1.8 %collective-permute-done.15 = bf16[32,2048]{1,0:T(8,128)(2,1)S(1)} collective-permute-done((bf16[32,2048]{1,0:T(8,128)(2,1)S(1)}, bf16[32,2048]{1,0:T(8,128)(2,1)S(1)}, u32[]{:S(2)}, u32[]{:S(2)}) %collective-permute-start.15) | collective-permute-done | bytes 131104 | tf_op jit(solution)/shard_map/ppermute | solution.py:25
  58.6 2.5 %collective-permute-start.16 = (bf16[32,2048]{1,0:T(8,128)(2,1)S(1)}, bf16[32,2048]{1,0:T(8,128)(2,1)S(1)}, u32[]{:S(2)}, u32[]{:S(2)}) collective-permute-start(bf16[32,2048]{1,0:T(8,128)(2,1)S(1)} %add_convert_fusion), channel_id=1, source_target_pairs={{0,6},{1,7},{2,4},{3,5},{4,2},{5,3},{6,0},{7,1},{8,14},{9,15},{10,... | collective-permute-start | bytes 393224 | tf_op jit(solution)/shard_map/ppermute | solution.py:25
  61.1 0.2 collective-permute-done.13
  61.4 0.7 collective-permute-start.14
  62.1 2.1 %collective-permute-done.11 = bf16[32,2048]{1,0:T(8,128)(2,1)S(1)} collective-permute-done((bf16[32,2048]{1,0:T(8,128)(2,1)S(1)}, bf16[32,2048]{1,0:T(8,128)(2,1)S(1)}, u32[]{:S(2)}, u32[]{:S(2)}) %collective-permute-start.11) | collective-permute-done | bytes 131104 | tf_op jit(solution)/shard_map/ppermute | solution.py:25
  64.2 0.4 collective-permute-start.12
  64.6 2.4 %collective-permute-done.10 = bf16[32,2048]{1,0:T(8,128)(2,1)S(1)} collective-permute-done((bf16[32,2048]{1,0:T(8,128)(2,1)S(1)}, bf16[32,2048]{1,0:T(8,128)(2,1)S(1)}, u32[]{:S(2)}, u32[]{:S(2)}) %collective-permute-start.10) | collective-permute-done | bytes 131104 | tf_op jit(solution)/shard_map/ppermute | solution.py:25
  67.0 0.0 collective-permute-done.16.refs_3_
  67.0 2.5 %collective-permute-done.14.refs_2_ = bf16[32,2048]{1,0:T(8,128)(2,1)S(1)} collective-permute-done((bf16[32,2048]{1,0:T(8,128)(2,1)S(1)}, bf16[32,2048]{1,0:T(8,128)(2,1)S(1)}, u32[]{:S(2)}, u32[]{:S(2)}) %collective-permute-start.14) | collective-permute-done | bytes 131104 | tf_op jit(solution)/shard_map/ppermute | solution.py:25
  69.5 1.0 %collective-permute-done.12.refs_1_ = bf16[32,2048]{1,0:T(8,128)(2,1)S(1)} collective-permute-done((bf16[32,2048]{1,0:T(8,128)(2,1)S(1)}, bf16[32,2048]{1,0:T(8,128)(2,1)S(1)}, u32[]{:S(2)}, u32[]{:S(2)}) %collective-permute-start.12) | collective-permute-done | bytes 131104 | tf_op jit(solution)/shard_map/ppermute | solution.py:25
  70.5 0.3 finish_tokens.1
  70.8 0.8 collective-permute-start.21
  71.6 0.0 collective-permute-done.20.refs_1_
  71.6 2.9 %collective-permute-done.21.refs_3_ = f32[8,128]{1,0:T(8,128)S(1)} collective-permute-done((f32[8,128]{1,0:T(8,128)S(1)}, f32[8,128]{1,0:T(8,128)S(1)}, u32[]{:S(2)}, u32[]{:S(2)}) %collective-permute-start.21) | collective-permute-done | bytes 4128 | tf_op jit(solution)/shard_map/ppermute | solution.py:25
  74.5 0.1 sum_seeds.1
  74.6 0.1 collective-permute-start.22
  74.6 3.2 %collective-permute-start.23 = (bf16[16,2176]{1,0:T(8,128)(2,1)S(1)}, bf16[16,2176]{1,0:T(8,128)(2,1)S(1)}, u32[]{:S(2)}, u32[]{:S(2)}) collective-permute-start(bf16[16,2176]{1,0:T(8,128)(2,1)S(1)} %get-tuple-element.87), channel_id=1, source_target_pairs={{0,4},{1,5},{2,6},{3,7},{4,0},{5,1},{6,2},{7,3},{8,12},{9,13},{10,... | collective-permute-start | bytes 208904 | tf_op jit(solution)/shard_map/ppermute | solution.py:25
  77.8 1.2 %collective-permute-start.24 = (bf16[16,2176]{1,0:T(8,128)(2,1)S(1)}, bf16[16,2176]{1,0:T(8,128)(2,1)S(1)}, u32[]{:S(2)}, u32[]{:S(2)}) collective-permute-start(bf16[16,2176]{1,0:T(8,128)(2,1)S(1)} %get-tuple-element.88), channel_id=1, source_target_pairs={{0,6},{1,7},{2,4},{3,5},{4,2},{5,3},{6,0},{7,1},{8,14},{9,15},{10,... | collective-permute-start | bytes 208904 | tf_op jit(solution)/shard_map/ppermute | solution.py:25
  79.0 0.0 collective-permute-start.17
  79.0 0.9 %collective-permute-start.18 = (bf16[8,2048]{1,0:T(8,128)(2,1)S(1)}, bf16[8,2048]{1,0:T(8,128)(2,1)S(1)}, u32[]{:S(2)}, u32[]{:S(2)}) collective-permute-start(bf16[8,2048]{1,0:T(8,128)(2,1)S(1)} %get-tuple-element.77), channel_id=1, source_target_pairs={{0,16},{8,24},{16,0},{24,8},{1,17},{9,25},{17,1},{25,9},{2,18},{10... | collective-permute-start | bytes 98312 | tf_op jit(solution)/shard_map/ppermute | solution.py:25
  79.9 0.3 collective-permute-done.17.refs_1_
  80.2 0.7 collective-permute-start.19
  80.9 2.1 %side.1 = (f32[1,1]{1,0:T(1,128)}, f32[1,4096]{1,0:T(1,128)}) custom-call(s32[2]{0:T(128)S(1)} %pad_add_fusion.group_ref.place_ref, bf16[256,2048]{1,0:T(8,128)(2,1)S(1)} %get-tuple-element.65.normed_ref, s32[1,128]{1,0:T(1,128)S(1)} %copy-done.3, f32[1,4096]{1,0:T(1,128)S(1)} %copy-done), custom_call_target="tpu_custom_call" | custom-call | tf_op jit(solution)/shard_map/side/pallas_call | solution.py:385
  83.0 0.0 collective-permute-done.18.refs_2_
  83.0 0.6 collective-permute-done.19.refs_3_
  83.6 1.2 %unpack.1 = bf16[4,8,2048]{2,1,0:T(8,128)(2,1)} custom-call(s32[2]{0:T(128)S(1)} %pad_add_fusion.group_ref.place_ref, bf16[8,2048]{1,0:T(8,128)(2,1)S(1)} %get-tuple-element.75.refs_0_, bf16[8,2048]{1,0:T(8,128)(2,1)S(1)} %collective-permute-done.17.refs_1_, bf16[8,2048]{1,0:T(8,128)(2,1)S(1)} %collective-permute-done.18.refs_2_, ...), custom_call_target="tpu_custom_call" | custom-call | tf_op jit(solution)/shard_map/unpack/pallas_call | solution.py:402
  84.8 0.0 collective-permute-done.22.refs_0_
  84.8 1.4 %finish_seeds.1 = (bf16[16,2048]{1,0:T(8,128)(2,1)}, f32[1,1]{1,0:T(1,128)}) custom-call(bf16[16,2048]{1,0:T(8,128)(2,1)S(1)} %get-tuple-element.79.features_ref, f32[1,2048]{1,0:T(1,128)S(1)} %copy-done.1, f32[1,1]{1,0:T(1,128)} %get-tuple-element.80.spread_ref, f32[16,2048]{1,0:T(8,128)S(1)} %get-tuple-element.84.mine_ref, ...), custom_call_target="tpu_custom_call" | custom-call | tf_op jit(solution)/shard_map/finish_seeds/pallas_call | solution.py:356
  (14 shorter events, 0.2 us)
Async XLA Ops:
  2.3 3.2 %collective-permute-start = (bf16[8,2176]{1,0:T(8,128)(2,1)S(1)}, bf16[8,2176]{1,0:T(8,128)(2,1)S(1)}, u32[]{:S(2)}, u32[]{:S(2)}) collective-permute-start(bf16[8,2176]{1,0:T(8,128)(2,1)S(1)} %get-tuple-element.50), channel_id=1, source_target_pairs={{0,8},{8,0},{16,24},{24,16},{1,9},{9,1},{17,25},{25,17},{2,10},{10... | collective-permute-start | bytes 104456 | tf_op jit(solution)/shard_map/ppermute | solution.py:25
  2.9 4.6 %collective-permute-start.1 = (bf16[8,2176]{1,0:T(8,128)(2,1)S(1)}, bf16[8,2176]{1,0:T(8,128)(2,1)S(1)}, u32[]{:S(2)}, u32[]{:S(2)}) collective-permute-start(bf16[8,2176]{1,0:T(8,128)(2,1)S(1)} %get-tuple-element.51), channel_id=1, source_target_pairs={{0,16},{8,24},{16,0},{24,8},{1,17},{9,25},{17,1},{25,9},{2,18},{10... | collective-permute-start | bytes 104456 | tf_op jit(solution)/shard_map/ppermute | solution.py:25
  5.4 3.4 %collective-permute-start.2 = (bf16[8,2176]{1,0:T(8,128)(2,1)S(1)}, bf16[8,2176]{1,0:T(8,128)(2,1)S(1)}, u32[]{:S(2)}, u32[]{:S(2)}) collective-permute-start(bf16[8,2176]{1,0:T(8,128)(2,1)S(1)} %get-tuple-element.52), channel_id=1, source_target_pairs={{0,24},{8,16},{16,8},{24,0},{1,25},{9,17},{17,9},{25,1},{2,26},{10... | collective-permute-start | bytes 104456 | tf_op jit(solution)/shard_map/ppermute | solution.py:25
  8.8 8.4 %collective-permute-start.3 = (bf16[32,2176]{1,0:T(8,128)(2,1)S(1)}, bf16[32,2176]{1,0:T(8,128)(2,1)S(1)}, u32[]{:S(2)}, u32[]{:S(2)}) collective-permute-start(bf16[32,2176]{1,0:T(8,128)(2,1)S(1)} %constant_dynamic-update-slice_fusion.after_ref.refs_3_), channel_id=1, source_target_pairs={{0,6},{1,7},{2,4},{3,5},{4,2},{5,3},{6,0},{7,1},{8,14},{9,15},{10,... | collective-permute-start | bytes 417800 | tf_op jit(solution)/shard_map/ppermute | solution.py:25
  12.4 8.1 %collective-permute-start.5 = (bf16[32,2176]{1,0:T(8,128)(2,1)S(1)}, bf16[32,2176]{1,0:T(8,128)(2,1)S(1)}, u32[]{:S(2)}, u32[]{:S(2)}) collective-permute-start(bf16[32,2176]{1,0:T(8,128)(2,1)S(1)} %constant_dynamic-update-slice_fusion.after_ref.refs_3_), channel_id=1, source_target_pairs={{0,2},{1,3},{2,0},{3,1},{4,6},{5,7},{6,4},{7,5},{8,10},{9,11},{10,... | collective-permute-start | bytes 417800 | tf_op jit(solution)/shard_map/ppermute | solution.py:25
  12.4 12.1 %collective-permute-start.7 = (bf16[32,2176]{1,0:T(8,128)(2,1)S(1)}, bf16[32,2176]{1,0:T(8,128)(2,1)S(1)}, u32[]{:S(2)}, u32[]{:S(2)}) collective-permute-start(bf16[32,2176]{1,0:T(8,128)(2,1)S(1)} %constant_dynamic-update-slice_fusion.after_ref.refs_3_), channel_id=1, source_target_pairs={{0,4},{1,5},{2,6},{3,7},{4,0},{5,1},{6,2},{7,3},{8,12},{9,13},{10,... | collective-permute-start | bytes 417800 | tf_op jit(solution)/shard_map/ppermute | solution.py:25
  13.2 25.4 %collective-permute-start.4 = (bf16[32,2176]{1,0:T(8,128)(2,1)S(1)}, bf16[32,2176]{1,0:T(8,128)(2,1)S(1)}, u32[]{:S(2)}, u32[]{:S(2)}) collective-permute-start(bf16[32,2176]{1,0:T(8,128)(2,1)S(1)} %constant_dynamic-update-slice_fusion.after_ref.refs_3_), channel_id=1, source_target_pairs={{0,1},{1,0},{2,3},{3,2},{4,5},{5,4},{6,7},{7,6},{8,9},{9,8},{10,11... | collective-permute-start | bytes 417800 | tf_op jit(solution)/shard_map/ppermute | solution.py:25
  17.2 21.5 %collective-permute-start.9 = (bf16[32,2176]{1,0:T(8,128)(2,1)S(1)}, bf16[32,2176]{1,0:T(8,128)(2,1)S(1)}, u32[]{:S(2)}, u32[]{:S(2)}) collective-permute-start(bf16[32,2176]{1,0:T(8,128)(2,1)S(1)} %collective-permute-done.3.after_ref.refs_9_), channel_id=1, source_target_pairs={{0,1},{1,0},{2,3},{3,2},{4,5},{5,4},{6,7},{7,6},{8,9},{9,8},{10,11... | collective-permute-start | bytes 417800 | tf_op jit(solution)/shard_map/ppermute | solution.py:25
  20.5 18.2 %collective-permute-start.6 = (bf16[32,2176]{1,0:T(8,128)(2,1)S(1)}, bf16[32,2176]{1,0:T(8,128)(2,1)S(1)}, u32[]{:S(2)}, u32[]{:S(2)}) collective-permute-start(bf16[32,2176]{1,0:T(8,128)(2,1)S(1)} %collective-permute-done.5.refs_5_), channel_id=1, source_target_pairs={{0,1},{1,0},{2,3},{3,2},{4,5},{5,4},{6,7},{7,6},{8,9},{9,8},{10,11... | collective-permute-start | bytes 417800 | tf_op jit(solution)/shard_map/ppermute | solution.py:25
  24.5 14.2 %collective-permute-start.8 = (bf16[32,2176]{1,0:T(8,128)(2,1)S(1)}, bf16[32,2176]{1,0:T(8,128)(2,1)S(1)}, u32[]{:S(2)}, u32[]{:S(2)}) collective-permute-start(bf16[32,2176]{1,0:T(8,128)(2,1)S(1)} %collective-permute-done.7.refs_7_), channel_id=1, source_target_pairs={{0,1},{1,0},{2,3},{3,2},{4,5},{5,4},{6,7},{7,6},{8,9},{9,8},{10,11... | collective-permute-start | bytes 417800 | tf_op jit(solution)/shard_map/ppermute | solution.py:25
  35.5 3.2 %copy-start.2 = (s32[1,128]{1,0:T(1,128)S(1)}, s32[1,128]{1,0:T(1,128)}, u32[]{:S(2)}) copy-start(s32[1,128]{1,0:T(1,128)} %seed_ref.1) | copy-start | bytes 1540
  38.6 31.9 %copy-start.1 = (f32[1,2048]{1,0:T(1,128)S(1)}, f32[1,2048]{1,0:T(1,128)}, u32[]{:S(2)}) copy-start(f32[1,2048]{1,0:T(1,128)} %dec_ref.3) | copy-start | bytes 24580
  38.7 42.2 %copy-start = (f32[1,4096]{1,0:T(1,128)S(1)}, f32[1,4096]{1,0:T(1,128)}, u32[]{:S(2)}) copy-start(f32[1,4096]{1,0:T(1,128)} %enc_ref.1) | copy-start | bytes 49156
  38.7 42.2 %copy-start.3 = (s32[1,128]{1,0:T(1,128)S(1)}, s32[1,128]{1,0:T(1,128)}, u32[]{:S(2)}) copy-start(s32[1,128]{1,0:T(1,128)} %dead_ref.1) | copy-start | bytes 1540
  52.1 6.4 %collective-permute-start.15 = (bf16[32,2048]{1,0:T(8,128)(2,1)S(1)}, bf16[32,2048]{1,0:T(8,128)(2,1)S(1)}, u32[]{:S(2)}, u32[]{:S(2)}) collective-permute-start(bf16[32,2048]{1,0:T(8,128)(2,1)S(1)} %get-tuple-element.74), channel_id=1, source_target_pairs={{0,1},{1,0},{2,3},{3,2},{4,5},{5,4},{6,7},{7,6},{8,9},{9,8},{10,11... | collective-permute-start | bytes 393224 | tf_op jit(solution)/shard_map/ppermute | solution.py:25
  52.7 8.7 %collective-permute-start.13 = (bf16[32,2048]{1,0:T(8,128)(2,1)S(1)}, bf16[32,2048]{1,0:T(8,128)(2,1)S(1)}, u32[]{:S(2)}, u32[]{:S(2)}) collective-permute-start(bf16[32,2048]{1,0:T(8,128)(2,1)S(1)} %get-tuple-element.72), channel_id=1, source_target_pairs={{0,1},{1,0},{2,3},{3,2},{4,5},{5,4},{6,7},{7,6},{8,9},{9,8},{10,11... | collective-permute-start | bytes 393224 | tf_op jit(solution)/shard_map/ppermute | solution.py:25
  54.2 10.0 %collective-permute-start.11 = (bf16[32,2048]{1,0:T(8,128)(2,1)S(1)}, bf16[32,2048]{1,0:T(8,128)(2,1)S(1)}, u32[]{:S(2)}, u32[]{:S(2)}) collective-permute-start(bf16[32,2048]{1,0:T(8,128)(2,1)S(1)} %get-tuple-element.70), channel_id=1, source_target_pairs={{0,1},{1,0},{2,3},{3,2},{4,5},{5,4},{6,7},{7,6},{8,9},{9,8},{10,11... | collective-permute-start | bytes 393224 | tf_op jit(solution)/shard_map/ppermute | solution.py:25
  54.7 12.3 %collective-permute-start.10 = (bf16[32,2048]{1,0:T(8,128)(2,1)S(1)}, bf16[32,2048]{1,0:T(8,128)(2,1)S(1)}, u32[]{:S(2)}, u32[]{:S(2)}) collective-permute-start(bf16[32,2048]{1,0:T(8,128)(2,1)S(1)} %get-tuple-element.68), channel_id=1, source_target_pairs={{0,1},{1,0},{2,3},{3,2},{4,5},{5,4},{6,7},{7,6},{8,9},{9,8},{10,11... | collective-permute-start | bytes 393224 | tf_op jit(solution)/shard_map/ppermute | solution.py:25
  56.2 15.4 %collective-permute-start.20 = (bf16[64,2048]{1,0:T(8,128)(2,1)S(1)}, bf16[64,2048]{1,0:T(8,128)(2,1)S(1)}, u32[]{:S(2)}, u32[]{:S(2)}) collective-permute-start(bf16[64,2048]{1,0:T(8,128)(2,1)S(1)} %get-tuple-element.82), channel_id=1, source_target_pairs={{0,1},{1,0},{2,3},{3,2},{4,5},{5,4},{6,7},{7,6},{8,9},{9,8},{10,11... | collective-permute-start | bytes 786440 | tf_op jit(solution)/shard_map/ppermute | solution.py:25
  58.6 8.4 %collective-permute-start.16 = (bf16[32,2048]{1,0:T(8,128)(2,1)S(1)}, bf16[32,2048]{1,0:T(8,128)(2,1)S(1)}, u32[]{:S(2)}, u32[]{:S(2)}) collective-permute-start(bf16[32,2048]{1,0:T(8,128)(2,1)S(1)} %add_convert_fusion), channel_id=1, source_target_pairs={{0,6},{1,7},{2,4},{3,5},{4,2},{5,3},{6,0},{7,1},{8,14},{9,15},{10,... | collective-permute-start | bytes 393224 | tf_op jit(solution)/shard_map/ppermute | solution.py:25
  61.4 8.1 %collective-permute-start.14 = (bf16[32,2048]{1,0:T(8,128)(2,1)S(1)}, bf16[32,2048]{1,0:T(8,128)(2,1)S(1)}, u32[]{:S(2)}, u32[]{:S(2)}) collective-permute-start(bf16[32,2048]{1,0:T(8,128)(2,1)S(1)} %add_convert_fusion.1), channel_id=1, source_target_pairs={{0,4},{1,5},{2,6},{3,7},{4,0},{5,1},{6,2},{7,3},{8,12},{9,13},{10,... | collective-permute-start | bytes 393224 | tf_op jit(solution)/shard_map/ppermute | solution.py:25
  64.2 6.3 %collective-permute-start.12 = (bf16[32,2048]{1,0:T(8,128)(2,1)S(1)}, bf16[32,2048]{1,0:T(8,128)(2,1)S(1)}, u32[]{:S(2)}, u32[]{:S(2)}) collective-permute-start(bf16[32,2048]{1,0:T(8,128)(2,1)S(1)} %add_convert_fusion.2), channel_id=1, source_target_pairs={{0,2},{1,3},{2,0},{3,1},{4,6},{5,7},{6,4},{7,5},{8,10},{9,11},{10,... | collective-permute-start | bytes 393224 | tf_op jit(solution)/shard_map/ppermute | solution.py:25
  70.8 3.7 %collective-permute-start.21 = (f32[8,128]{1,0:T(8,128)S(1)}, f32[8,128]{1,0:T(8,128)S(1)}, u32[]{:S(2)}, u32[]{:S(2)}) collective-permute-start(f32[8,128]{1,0:T(8,128)S(1)} %get-tuple-element.83.refs_2_), channel_id=1, source_target_pairs={{0,1},{1,0},{2,3},{3,2},{4,5},{5,4},{6,7},{7,6},{8,9},{9,8},{10,11... | collective-permute-start | bytes 12296 | tf_op jit(solution)/shard_map/ppermute | solution.py:25
  74.6 10.2 %collective-permute-start.22 = (bf16[16,2176]{1,0:T(8,128)(2,1)S(1)}, bf16[16,2176]{1,0:T(8,128)(2,1)S(1)}, u32[]{:S(2)}, u32[]{:S(2)}) collective-permute-start(bf16[16,2176]{1,0:T(8,128)(2,1)S(1)} %get-tuple-element.86), channel_id=1, source_target_pairs={{0,2},{1,3},{2,0},{3,1},{4,6},{5,7},{6,4},{7,5},{8,10},{9,11},{10,... | collective-permute-start | bytes 208904 | tf_op jit(solution)/shard_map/ppermute | solution.py:25
  74.6 10.1 %collective-permute-start.23 = (bf16[16,2176]{1,0:T(8,128)(2,1)S(1)}, bf16[16,2176]{1,0:T(8,128)(2,1)S(1)}, u32[]{:S(2)}, u32[]{:S(2)}) collective-permute-start(bf16[16,2176]{1,0:T(8,128)(2,1)S(1)} %get-tuple-element.87), channel_id=1, source_target_pairs={{0,4},{1,5},{2,6},{3,7},{4,0},{5,1},{6,2},{7,3},{8,12},{9,13},{10,... | collective-permute-start | bytes 208904 | tf_op jit(solution)/shard_map/ppermute | solution.py:25
  77.8 7.0 %collective-permute-start.24 = (bf16[16,2176]{1,0:T(8,128)(2,1)S(1)}, bf16[16,2176]{1,0:T(8,128)(2,1)S(1)}, u32[]{:S(2)}, u32[]{:S(2)}) collective-permute-start(bf16[16,2176]{1,0:T(8,128)(2,1)S(1)} %get-tuple-element.88), channel_id=1, source_target_pairs={{0,6},{1,7},{2,4},{3,5},{4,2},{5,3},{6,0},{7,1},{8,14},{9,15},{10,... | collective-permute-start | bytes 208904 | tf_op jit(solution)/shard_map/ppermute | solution.py:25
  79.0 1.2 %collective-permute-start.17 = (bf16[8,2048]{1,0:T(8,128)(2,1)S(1)}, bf16[8,2048]{1,0:T(8,128)(2,1)S(1)}, u32[]{:S(2)}, u32[]{:S(2)}) collective-permute-start(bf16[8,2048]{1,0:T(8,128)(2,1)S(1)} %get-tuple-element.76), channel_id=1, source_target_pairs={{0,8},{8,0},{16,24},{24,16},{1,9},{9,1},{17,25},{25,17},{2,10},{10... | collective-permute-start | bytes 98312 | tf_op jit(solution)/shard_map/ppermute | solution.py:25
  79.0 3.9 %collective-permute-start.18 = (bf16[8,2048]{1,0:T(8,128)(2,1)S(1)}, bf16[8,2048]{1,0:T(8,128)(2,1)S(1)}, u32[]{:S(2)}, u32[]{:S(2)}) collective-permute-start(bf16[8,2048]{1,0:T(8,128)(2,1)S(1)} %get-tuple-element.77), channel_id=1, source_target_pairs={{0,16},{8,24},{16,0},{24,8},{1,17},{9,25},{17,1},{25,9},{2,18},{10... | collective-permute-start | bytes 98312 | tf_op jit(solution)/shard_map/ppermute | solution.py:25
  80.2 3.3 %collective-permute-start.19 = (bf16[8,2048]{1,0:T(8,128)(2,1)S(1)}, bf16[8,2048]{1,0:T(8,128)(2,1)S(1)}, u32[]{:S(2)}, u32[]{:S(2)}) collective-permute-start(bf16[8,2048]{1,0:T(8,128)(2,1)S(1)} %get-tuple-element.78), channel_id=1, source_target_pairs={{0,24},{8,16},{16,8},{24,0},{1,25},{9,17},{17,9},{25,1},{2,26},{10... | collective-permute-start | bytes 98312 | tf_op jit(solution)/shard_map/ppermute | solution.py:25

commit v3 on v2

--- a/solution.py
+++ b/solution.py
@@ -33,46 +33,43 @@
     return pltpu.with_memory_space_constraint(value, pltpu.HBM)
 
 
-def pack_kernel(groups, per_shard, lat_dev, group_ref, res_hbm, slots_hbm, *refs):
-    outs, (res_ref, slots_ref, sems) = refs[:groups], refs[groups:]
+def pack_kernel(groups, per_shard, lat_dev, place_ref, res_hbm, slots_hbm, *refs):
+    outs, (slots_ref, sems) = refs[:groups], refs[groups:]
+    layers = [jnp.bitwise_xor(place_ref[1], mask) for mask in range(groups)]
+    width = res_hbm.shape[2]
+    slot_count = slots_ref.shape[2]
+    slot_copy = pltpu.make_async_copy(slots_hbm, slots_ref, sems.at[groups])
+    slot_copy.start()
     copies = [
-        pltpu.make_async_copy(slots_hbm, slots_ref, sems.at[0]),
-        pltpu.make_async_copy(res_hbm, res_ref, sems.at[1]),
+        pltpu.make_async_copy(res_hbm.at[layer], out.at[:, pl.ds(0, width)], sems.at[mask])
+        for mask, (layer, out) in enumerate(zip(layers, outs))
     ]
     for copy in copies:
         copy.start()
-    for copy in copies:
-        copy.wait()
-    group = group_ref[1]
-    width = res_ref.shape[2]
-    slot_count = slots_ref.shape[2]
+    slot_copy.wait()
     shard = lax.broadcasted_iota(jnp.int32, slots_ref.shape[1:], 1) // per_shard
-    for mask in range(groups):
-        layer = jnp.bitwise_xor(group, mask)
+    for layer, out in zip(layers, outs):
         slots = slots_ref[layer]
         live = slots >= 0
         local = slots - shard * lat_dev
         high = jnp.where(live, local // LOW, -1)
         low = jnp.where(live, local % LOW, 0)
-        outs[mask][:, :width] = res_ref[layer]
-        outs[mask][:, width : width + 2 * slot_count] = jnp.concatenate([high, low], axis=1).astype(F32).astype(BF16)
-
-
-def pack(group, residuals, slots, per_shard, lat_dev):
+        out[:, width : width + 2 * slot_count] = jnp.concatenate([high, low], axis=1).astype(F32).astype(BF16)
+    for copy in copies:
+        copy.wait()
+
+
+def pack(place, residuals, slots, per_shard, lat_dev):
     groups, rows, width = residuals.shape
     return pl.pallas_call(
         functools.partial(pack_kernel, groups, per_shard, lat_dev),
         out_shape=[pltpu.VMEM((rows, width + 2 * slots.shape[2]), BF16)] * groups,
         in_specs=[SMEM_SPEC, HBM_SPEC, HBM_SPEC],
         out_specs=[VMEM_SPEC] * groups,
-        scratch_shapes=[
-            pltpu.VMEM(residuals.shape, residuals.dtype),
-            pltpu.VMEM(slots.shape, slots.dtype),
-            pltpu.SemaphoreType.DMA((2,)),
-        ],
+        scratch_shapes=[pltpu.VMEM(slots.shape, slots.dtype), pltpu.SemaphoreType.DMA((groups + 1,))],
         compiler_params=pltpu.CompilerParams(vmem_limit_bytes=4 << 20),
         name="pack",
-    )(group, in_hbm(residuals), in_hbm(slots))
+    )(place, in_hbm(residuals), in_hbm(slots))
 
 
 def lane_to_line(column):
@@ -409,9 +406,6 @@
     )(group, *[in_vmem(part) for part in parts])
 
 
-LOADS = 4
-
-
 def body(residuals, topk_slots, dictionary, enc_bias, dec_bias, dead_ids, seed_tokens):
     tok_dev = residuals.shape[1]
     lat_count = lax.axis_size("lat")
@@ -431,12 +425,12 @@
     columns = [mine] + [lat(mine, inner * z) for z in range(1, outer)]
     blocks = [block for column in columns for block in [column] + [lat(column, x) for x in range(1, inner)]]
 
-    part_rows = lat_dev // LOADS
-    loaded = ()
-    for part, after in enumerate((packed[0], mine, columns[-1], columns[-1])):
-        loaded = load(loaded, after, dictionary[0], enc_bias, dec_bias, part * part_rows, part_rows, part_rows // 4)
+    loaded, first = (), 0
+    for after, rows in ((mine, lat_dev // 2), (columns[-1], lat_dev // 2)):
+        loaded = load(loaded, after, dictionary[0], enc_bias, dec_bias, first, rows, lat_dev // 16)
+        first += rows
     shares, seed_shares, (normed, seed_features, norm_part, mass) = main(
-        place, seed_tokens, loaded, blocks, outer, tok_dev, per_shard, slot_count, 1024, 1024
+        place, seed_tokens, loaded, blocks, outer, tok_dev, per_shard, slot_count, 2048, 1024
     )
 
     sums = [None] * outer

time: 86.5 us -> 83.3 us (0.963)
  Pallas kernels: 32.6 us -> 29.4 us
    pallas_call x4 -> x2, Pallas kernels: 12.6 us -> 9.98 us  [load(): pl.pallas_call(functools.partial(load_kernel, first, rows, tile), out_sha...]
  transfers between devices with their start and end apart: 25 -> 25, of which waited for: 14 -> 14; matrix products, arithmetic and copies ran while one was open for 0% -> 0% of each run, Pallas kernels for 19% -> 16%
where the time goes in v3:
time: 83.3 us; the launch traced here: 83 us
  Pallas kernels  29.4 us (35%)
  starting transfers between devices  28.6 us (34%)
  waiting for transfers between devices  23.9 us (29%)
    ppermute x25, starting transfers between devices, shift_to(): return lax.ppermute(value, axis, [(i, i ^ mask) for i in range(size)])  28.6 us
    ppermute x25, waiting for transfers between devices, shift_to(): return lax.ppermute(value, axis, [(i, i ^ mask) for i in range(size)])  23.9 us
    pallas_call x1, Pallas kernels, main(): pl.pallas_call(functools.partial(main_kernel, parts, count, outer, chunk,...  12.9 us
    pallas_call x2, Pallas kernels, load(): pl.pallas_call(functools.partial(load_kernel, first, rows, tile), out_sha...  9.98 us
    pallas_call x1, Pallas kernels, side(): pl.pallas_call(functools.partial(side_kernel, 256), out_shape=[pltpu.VMEM...  2.08 us
  transfers between devices with their start and end apart: 25, of which 14 were waited for; matrix products, arithmetic and copies ran while one was open for 0% of the time, Pallas kernels for 16%

profile of v3, /device:TPU:0, one launch (start us, length us, event | category | flops | bytes accessed | tf_op | source)
XLA Modules:
  0.0 83.0 jit_solution(9279270601305192269)
XLA Ops:
  0.6 0.1 pad_add_fusion.place_ref.group_ref
  0.7 1.4 %pack.1 = (bf16[8,2176]{1,0:T(8,128)(2,1)S(1)}, bf16[8,2176]{1,0:T(8,128)(2,1)S(1)}, bf16[8,2176]{1,0:T(8,128)(2,1)S(1)}, bf16[8,2176]{1,0:T(8,128)(2,1)S(1)}) custom-call(s32[2]{0:T(128)S(1)} %pad_add_fusion.place_ref.group_ref, bf16[4,8,2048]{2,1,0:T(8,128)(2,1)} %res_hbm.1, s32[4,8,64]{2,1,0:T(8,128)} %slots_hbm.1), custom_call_target="tpu_custom_call" | custom-call | tf_op jit(solution)/shard_map/pack/pallas_call | solution.py:64
  2.1 0.6 collective-permute-start
  2.7 2.6 %collective-permute-start.1 = (bf16[8,2176]{1,0:T(8,128)(2,1)S(1)}, bf16[8,2176]{1,0:T(8,128)(2,1)S(1)}, u32[]{:S(2)}, u32[]{:S(2)}) collective-permute-start(bf16[8,2176]{1,0:T(8,128)(2,1)S(1)} %get-tuple-element.45), channel_id=1, source_target_pairs={{0,16},{8,24},{16,0},{24,8},{1,17},{9,25},{17,1},{25,9},{2,18},{10... | collective-permute-start | bytes 104456 | tf_op jit(solution)/shard_map/ppermute | solution.py:25
  5.3 0.0 collective-permute-start.2
  5.3 0.0 collective-permute-done
  5.3 2.0 %collective-permute-done.1 = bf16[8,2176]{1,0:T(8,128)(2,1)S(1)} collective-permute-done((bf16[8,2176]{1,0:T(8,128)(2,1)S(1)}, bf16[8,2176]{1,0:T(8,128)(2,1)S(1)}, u32[]{:S(2)}, u32[]{:S(2)}) %collective-permute-start.1) | collective-permute-done | bytes 34848 | tf_op jit(solution)/shard_map/ppermute | solution.py:25
  7.3 1.4 %collective-permute-done.2 = bf16[8,2176]{1,0:T(8,128)(2,1)S(1)} collective-permute-done((bf16[8,2176]{1,0:T(8,128)(2,1)S(1)}, bf16[8,2176]{1,0:T(8,128)(2,1)S(1)}, u32[]{:S(2)}, u32[]{:S(2)}) %collective-permute-start.2) | collective-permute-done | bytes 34848 | tf_op jit(solution)/shard_map/ppermute | solution.py:25
  8.7 3.6 %collective-permute-start.3 = (bf16[32,2176]{1,0:T(8,128)(2,1)S(1)}, bf16[32,2176]{1,0:T(8,128)(2,1)S(1)}, u32[]{:S(2)}, u32[]{:S(2)}) collective-permute-start(bf16[32,2176]{1,0:T(8,128)(2,1)S(1)} %constant_dynamic-update-slice_fusion.after_ref.refs_3_), channel_id=1, source_target_pairs={{0,6},{1,7},{2,4},{3,5},{4,2},{5,3},{6,0},{7,1},{8,14},{9,15},{10,... | collective-permute-start | bytes 417800 | tf_op jit(solution)/shard_map/ppermute | solution.py:25
  12.3 0.0 collective-permute-start.5
  12.3 0.8 collective-permute-start.7
  13.1 1.5 %collective-permute-start.4 = (bf16[32,2176]{1,0:T(8,128)(2,1)S(1)}, bf16[32,2176]{1,0:T(8,128)(2,1)S(1)}, u32[]{:S(2)}, u32[]{:S(2)}) collective-permute-start(bf16[32,2176]{1,0:T(8,128)(2,1)S(1)} %constant_dynamic-update-slice_fusion.after_ref.refs_3_), channel_id=1, source_target_pairs={{0,1},{1,0},{2,3},{3,2},{4,5},{5,4},{6,7},{7,6},{8,9},{9,8},{10,11... | collective-permute-start | bytes 417800 | tf_op jit(solution)/shard_map/ppermute | solution.py:25
  14.6 2.5 %collective-permute-done.3.after_ref.refs_9_ = bf16[32,2176]{1,0:T(8,128)(2,1)S(1)} collective-permute-done((bf16[32,2176]{1,0:T(8,128)(2,1)S(1)}, bf16[32,2176]{1,0:T(8,128)(2,1)S(1)}, u32[]{:S(2)}, u32[]{:S(2)}) %collective-permute-start.3) | collective-permute-done | bytes 139296 | tf_op jit(solution)/shard_map/ppermute | solution.py:25
  17.1 1.5 %collective-permute-start.9 = (bf16[32,2176]{1,0:T(8,128)(2,1)S(1)}, bf16[32,2176]{1,0:T(8,128)(2,1)S(1)}, u32[]{:S(2)}, u32[]{:S(2)}) collective-permute-start(bf16[32,2176]{1,0:T(8,128)(2,1)S(1)} %collective-permute-done.3.after_ref.refs_9_), channel_id=1, source_target_pairs={{0,1},{1,0},{2,3},{3,2},{4,5},{5,4},{6,7},{7,6},{8,9},{9,8},{10,11... | collective-permute-start | bytes 417800 | tf_op jit(solution)/shard_map/ppermute | solution.py:25
  18.6 1.8 %collective-permute-done.5.refs_5_ = bf16[32,2176]{1,0:T(8,128)(2,1)S(1)} collective-permute-done((bf16[32,2176]{1,0:T(8,128)(2,1)S(1)}, bf16[32,2176]{1,0:T(8,128)(2,1)S(1)}, u32[]{:S(2)}, u32[]{:S(2)}) %collective-permute-start.5) | collective-permute-done | bytes 139296 | tf_op jit(solution)/shard_map/ppermute | solution.py:25
  20.3 1.5 %collective-permute-start.6 = (bf16[32,2176]{1,0:T(8,128)(2,1)S(1)}, bf16[32,2176]{1,0:T(8,128)(2,1)S(1)}, u32[]{:S(2)}, u32[]{:S(2)}) collective-permute-start(bf16[32,2176]{1,0:T(8,128)(2,1)S(1)} %collective-permute-done.5.refs_5_), channel_id=1, source_target_pairs={{0,1},{1,0},{2,3},{3,2},{4,5},{5,4},{6,7},{7,6},{8,9},{9,8},{10,11... | collective-permute-start | bytes 417800 | tf_op jit(solution)/shard_map/ppermute | solution.py:25
  21.8 2.5 %collective-permute-done.7.refs_7_ = bf16[32,2176]{1,0:T(8,128)(2,1)S(1)} collective-permute-done((bf16[32,2176]{1,0:T(8,128)(2,1)S(1)}, bf16[32,2176]{1,0:T(8,128)(2,1)S(1)}, u32[]{:S(2)}, u32[]{:S(2)}) %collective-permute-start.7) | collective-permute-done | bytes 139296 | tf_op jit(solution)/shard_map/ppermute | solution.py:25
  24.4 1.5 %collective-permute-start.8 = (bf16[32,2176]{1,0:T(8,128)(2,1)S(1)}, bf16[32,2176]{1,0:T(8,128)(2,1)S(1)}, u32[]{:S(2)}, u32[]{:S(2)}) collective-permute-start(bf16[32,2176]{1,0:T(8,128)(2,1)S(1)} %collective-permute-done.7.refs_7_), channel_id=1, source_target_pairs={{0,1},{1,0},{2,3},{3,2},{4,5},{5,4},{6,7},{7,6},{8,9},{9,8},{10,11... | collective-permute-start | bytes 417800 | tf_op jit(solution)/shard_map/ppermute | solution.py:25
  25.9 5.0 %load.2 = (bf16[4096,2048]{1,0:T(8,128)(2,1)S(1)}, f32[2,4096]{1,0:T(2,128)S(1)}, f32[8,128]{1,0:T(8,128)S(1)}) custom-call(bf16[32,2176]{1,0:T(8,128)(2,1)S(1)} %constant_dynamic-update-slice_fusion.after_ref.refs_3_, bf16[4096,2048]{1,0:T(8,128)(2,1)} %bitcast.5, f32[1,4096]{1,0:T(1,128)} %enc_ref.1, f32[1,2048]{1,0:T(1,128)} %dec_ref.3), custom_call_target="tpu_custom_call" | custom-call | tf_op jit(solution)/shard_map/load/pallas_call | solution.py:110
  30.9 0.0 copy-start.2
  30.9 5.0 %load.3 = (bf16[4096,2048]{1,0:T(8,128)(2,1)S(1)}, f32[2,4096]{1,0:T(2,128)S(1)}, f32[8,128]{1,0:T(8,128)S(1)}) custom-call(bf16[32,2176]{1,0:T(8,128)(2,1)S(1)} %collective-permute-done.3.after_ref.refs_9_, bf16[4096,2048]{1,0:T(8,128)(2,1)} %bitcast.6, f32[1,4096]{1,0:T(1,128)} %enc_ref.1, ...), custom_call_target="tpu_custom_call", output_to_operand_aliasing={{0}: (4, {}), {1}: (5, {}), {2}: (6, {})} | custom-call | tf_op jit(solution)/shard_map/load/pallas_call | solution.py:110
  35.9 0.0 copy-start.1
  35.9 0.0 copy-start
  35.9 0.0 copy-start.3
  35.9 0.0 collective-permute-done.4.refs_4_
  35.9 0.0 collective-permute-done.9.refs_10_
  35.9 0.0 collective-permute-done.6.refs_6_
  35.9 0.0 collective-permute-done.8.refs_8_
  36.0 12.9 %sparse_code.1 = (bf16[32,2048]{1,0:T(8,128)(2,1)S(1)}, bf16[32,2048]{1,0:T(8,128)(2,1)S(1)}, bf16[32,2048]{1,0:T(8,128)(2,1)S(1)}, bf16[32,2048]{1,0:T(8,128)(2...) custom-call(s32[2]{0:T(128)S(1)} %pad_add_fusion.place_ref.group_ref, ...), custom_call_target="tpu_custom_call" | custom-call | tf_op jit(solution)/shard_map/sparse_code/pallas_call | solution.py:243
  48.9 0.5 collective-permute-start.15
  49.4 1.5 %collective-permute-start.13 = (bf16[32,2048]{1,0:T(8,128)(2,1)S(1)}, bf16[32,2048]{1,0:T(8,128)(2,1)S(1)}, u32[]{:S(2)}, u32[]{:S(2)}) collective-permute-start(bf16[32,2048]{1,0:T(8,128)(2,1)S(1)} %get-tuple-element.60), channel_id=1, source_target_pairs={{0,1},{1,0},{2,3},{3,2},{4,5},{5,4},{6,7},{7,6},{8,9},{9,8},{10,11... | collective-permute-start | bytes 393224 | tf_op jit(solution)/shard_map/ppermute | solution.py:25
  50.9 0.5 collective-permute-start.11
  51.4 1.5 %collective-permute-start.10 = (bf16[32,2048]{1,0:T(8,128)(2,1)S(1)}, bf16[32,2048]{1,0:T(8,128)(2,1)S(1)}, u32[]{:S(2)}, u32[]{:S(2)}) collective-permute-start(bf16[32,2048]{1,0:T(8,128)(2,1)S(1)} %get-tuple-element.56), channel_id=1, source_target_pairs={{0,1},{1,0},{2,3},{3,2},{4,5},{5,4},{6,7},{7,6},{8,9},{9,8},{10,11... | collective-permute-start | bytes 393224 | tf_op jit(solution)/shard_map/ppermute | solution.py:25
  52.9 0.5 collective-permute-start.20
  53.5 1.8 %collective-permute-done.15 = bf16[32,2048]{1,0:T(8,128)(2,1)S(1)} collective-permute-done((bf16[32,2048]{1,0:T(8,128)(2,1)S(1)}, bf16[32,2048]{1,0:T(8,128)(2,1)S(1)}, u32[]{:S(2)}, u32[]{:S(2)}) %collective-permute-start.15) | collective-permute-done | bytes 131104 | tf_op jit(solution)/shard_map/ppermute | solution.py:25
  55.3 2.5 %collective-permute-start.16 = (bf16[32,2048]{1,0:T(8,128)(2,1)S(1)}, bf16[32,2048]{1,0:T(8,128)(2,1)S(1)}, u32[]{:S(2)}, u32[]{:S(2)}) collective-permute-start(bf16[32,2048]{1,0:T(8,128)(2,1)S(1)} %add_convert_fusion), channel_id=1, source_target_pairs={{0,6},{1,7},{2,4},{3,5},{4,2},{5,3},{6,0},{7,1},{8,14},{9,15},{10,... | collective-permute-start | bytes 393224 | tf_op jit(solution)/shard_map/ppermute | solution.py:25
  57.8 0.2 collective-permute-done.13
  58.1 0.7 collective-permute-start.14
  58.8 2.0 %collective-permute-done.11 = bf16[32,2048]{1,0:T(8,128)(2,1)S(1)} collective-permute-done((bf16[32,2048]{1,0:T(8,128)(2,1)S(1)}, bf16[32,2048]{1,0:T(8,128)(2,1)S(1)}, u32[]{:S(2)}, u32[]{:S(2)}) %collective-permute-start.11) | collective-permute-done | bytes 131104 | tf_op jit(solution)/shard_map/ppermute | solution.py:25
  60.9 0.4 collective-permute-start.12
  61.3 2.4 %collective-permute-done.10 = bf16[32,2048]{1,0:T(8,128)(2,1)S(1)} collective-permute-done((bf16[32,2048]{1,0:T(8,128)(2,1)S(1)}, bf16[32,2048]{1,0:T(8,128)(2,1)S(1)}, u32[]{:S(2)}, u32[]{:S(2)}) %collective-permute-start.10) | collective-permute-done | bytes 131104 | tf_op jit(solution)/shard_map/ppermute | solution.py:25
  63.7 0.0 collective-permute-done.16.refs_3_
  63.7 2.5 %collective-permute-done.14.refs_2_ = bf16[32,2048]{1,0:T(8,128)(2,1)S(1)} collective-permute-done((bf16[32,2048]{1,0:T(8,128)(2,1)S(1)}, bf16[32,2048]{1,0:T(8,128)(2,1)S(1)}, u32[]{:S(2)}, u32[]{:S(2)}) %collective-permute-start.14) | collective-permute-done | bytes 131104 | tf_op jit(solution)/shard_map/ppermute | solution.py:25
  66.2 1.0 %collective-permute-done.12.refs_1_ = bf16[32,2048]{1,0:T(8,128)(2,1)S(1)} collective-permute-done((bf16[32,2048]{1,0:T(8,128)(2,1)S(1)}, bf16[32,2048]{1,0:T(8,128)(2,1)S(1)}, u32[]{:S(2)}, u32[]{:S(2)}) %collective-permute-start.12) | collective-permute-done | bytes 131104 | tf_op jit(solution)/shard_map/ppermute | solution.py:25
  67.2 0.3 finish_tokens.1
  67.5 0.8 collective-permute-start.21
  68.3 0.0 collective-permute-done.20.refs_1_
  68.3 2.9 %collective-permute-done.21.refs_3_ = f32[8,128]{1,0:T(8,128)S(1)} collective-permute-done((f32[8,128]{1,0:T(8,128)S(1)}, f32[8,128]{1,0:T(8,128)S(1)}, u32[]{:S(2)}, u32[]{:S(2)}) %collective-permute-start.21) | collective-permute-done | bytes 4128 | tf_op jit(solution)/shard_map/ppermute | solution.py:25
  71.2 0.1 sum_seeds.1
  71.3 0.1 collective-permute-start.22
  71.4 3.2 %collective-permute-start.23 = (bf16[16,2176]{1,0:T(8,128)(2,1)S(1)}, bf16[16,2176]{1,0:T(8,128)(2,1)S(1)}, u32[]{:S(2)}, u32[]{:S(2)}) collective-permute-start(bf16[16,2176]{1,0:T(8,128)(2,1)S(1)} %get-tuple-element.75), channel_id=1, source_target_pairs={{0,4},{1,5},{2,6},{3,7},{4,0},{5,1},{6,2},{7,3},{8,12},{9,13},{10,... | collective-permute-start | bytes 208904 | tf_op jit(solution)/shard_map/ppermute | solution.py:25
  74.5 1.2 %collective-permute-start.24 = (bf16[16,2176]{1,0:T(8,128)(2,1)S(1)}, bf16[16,2176]{1,0:T(8,128)(2,1)S(1)}, u32[]{:S(2)}, u32[]{:S(2)}) collective-permute-start(bf16[16,2176]{1,0:T(8,128)(2,1)S(1)} %get-tuple-element.76), channel_id=1, source_target_pairs={{0,6},{1,7},{2,4},{3,5},{4,2},{5,3},{6,0},{7,1},{8,14},{9,15},{10,... | collective-permute-start | bytes 208904 | tf_op jit(solution)/shard_map/ppermute | solution.py:25
  75.7 0.0 collective-permute-start.17
  75.7 0.9 %collective-permute-start.18 = (bf16[8,2048]{1,0:T(8,128)(2,1)S(1)}, bf16[8,2048]{1,0:T(8,128)(2,1)S(1)}, u32[]{:S(2)}, u32[]{:S(2)}) collective-permute-start(bf16[8,2048]{1,0:T(8,128)(2,1)S(1)} %get-tuple-element.65), channel_id=1, source_target_pairs={{0,16},{8,24},{16,0},{24,8},{1,17},{9,25},{17,1},{25,9},{2,18},{10... | collective-permute-start | bytes 98312 | tf_op jit(solution)/shard_map/ppermute | solution.py:25
  76.6 0.3 collective-permute-done.17.refs_1_
  76.9 0.7 collective-permute-start.19
  77.6 2.1 %side.1 = (f32[1,1]{1,0:T(1,128)}, f32[1,4096]{1,0:T(1,128)}) custom-call(s32[2]{0:T(128)S(1)} %pad_add_fusion.place_ref.group_ref, bf16[256,2048]{1,0:T(8,128)(2,1)S(1)} %get-tuple-element.53.normed_ref, s32[1,128]{1,0:T(1,128)S(1)} %copy-done.3, f32[1,4096]{1,0:T(1,128)S(1)} %copy-done), custom_call_target="tpu_custom_call" | custom-call | tf_op jit(solution)/shard_map/side/pallas_call | solution.py:382
  79.7 0.0 collective-permute-done.18.refs_2_
  79.7 0.6 collective-permute-done.19.refs_3_
  80.3 1.2 %unpack.1 = bf16[4,8,2048]{2,1,0:T(8,128)(2,1)} custom-call(s32[2]{0:T(128)S(1)} %pad_add_fusion.place_ref.group_ref, bf16[8,2048]{1,0:T(8,128)(2,1)S(1)} %get-tuple-element.63.refs_0_, bf16[8,2048]{1,0:T(8,128)(2,1)S(1)} %collective-permute-done.17.refs_1_, bf16[8,2048]{1,0:T(8,128)(2,1)S(1)} %collective-permute-done.18.refs_2_, ...), custom_call_target="tpu_custom_call" | custom-call | tf_op jit(solution)/shard_map/unpack/pallas_call | solution.py:399
  81.5 0.0 collective-permute-done.22.refs_0_
  81.5 0.0 collective-permute-done.23.refs_1_
  81.5 0.0 collective-permute-done.24.refs_2_
  81.5 1.5 %finish_seeds.1 = (bf16[16,2048]{1,0:T(8,128)(2,1)}, f32[1,1]{1,0:T(1,128)}) custom-call(bf16[16,2048]{1,0:T(8,128)(2,1)S(1)} %get-tuple-element.67.features_ref, f32[1,2048]{1,0:T(1,128)S(1)} %copy-done.1, f32[1,1]{1,0:T(1,128)} %get-tuple-element.68.spread_ref, f32[16,2048]{1,0:T(8,128)S(1)} %get-tuple-element.72.mine_ref, ...), custom_call_target="tpu_custom_call" | custom-call | tf_op jit(solution)/shard_map/finish_seeds/pallas_call | solution.py:353
  (12 shorter events, 0.2 us)
Async XLA Ops:
  2.1 3.2 %collective-permute-start = (bf16[8,2176]{1,0:T(8,128)(2,1)S(1)}, bf16[8,2176]{1,0:T(8,128)(2,1)S(1)}, u32[]{:S(2)}, u32[]{:S(2)}) collective-permute-start(bf16[8,2176]{1,0:T(8,128)(2,1)S(1)} %get-tuple-element.44), channel_id=1, source_target_pairs={{0,8},{8,0},{16,24},{24,16},{1,9},{9,1},{17,25},{25,17},{2,10},{10... | collective-permute-start | bytes 104456 | tf_op jit(solution)/shard_map/ppermute | solution.py:25
  2.7 4.6 %collective-permute-start.1 = (bf16[8,2176]{1,0:T(8,128)(2,1)S(1)}, bf16[8,2176]{1,0:T(8,128)(2,1)S(1)}, u32[]{:S(2)}, u32[]{:S(2)}) collective-permute-start(bf16[8,2176]{1,0:T(8,128)(2,1)S(1)} %get-tuple-element.45), channel_id=1, source_target_pairs={{0,16},{8,24},{16,0},{24,8},{1,17},{9,25},{17,1},{25,9},{2,18},{10... | collective-permute-start | bytes 104456 | tf_op jit(solution)/shard_map/ppermute | solution.py:25
  5.3 3.4 %collective-permute-start.2 = (bf16[8,2176]{1,0:T(8,128)(2,1)S(1)}, bf16[8,2176]{1,0:T(8,128)(2,1)S(1)}, u32[]{:S(2)}, u32[]{:S(2)}) collective-permute-start(bf16[8,2176]{1,0:T(8,128)(2,1)S(1)} %get-tuple-element.46), channel_id=1, source_target_pairs={{0,24},{8,16},{16,8},{24,0},{1,25},{9,17},{17,9},{25,1},{2,26},{10... | collective-permute-start | bytes 104456 | tf_op jit(solution)/shard_map/ppermute | solution.py:25
  8.7 8.4 %collective-permute-start.3 = (bf16[32,2176]{1,0:T(8,128)(2,1)S(1)}, bf16[32,2176]{1,0:T(8,128)(2,1)S(1)}, u32[]{:S(2)}, u32[]{:S(2)}) collective-permute-start(bf16[32,2176]{1,0:T(8,128)(2,1)S(1)} %constant_dynamic-update-slice_fusion.after_ref.refs_3_), channel_id=1, source_target_pairs={{0,6},{1,7},{2,4},{3,5},{4,2},{5,3},{6,0},{7,1},{8,14},{9,15},{10,... | collective-permute-start | bytes 417800 | tf_op jit(solution)/shard_map/ppermute | solution.py:25
  12.3 8.1 %collective-permute-start.5 = (bf16[32,2176]{1,0:T(8,128)(2,1)S(1)}, bf16[32,2176]{1,0:T(8,128)(2,1)S(1)}, u32[]{:S(2)}, u32[]{:S(2)}) collective-permute-start(bf16[32,2176]{1,0:T(8,128)(2,1)S(1)} %constant_dynamic-update-slice_fusion.after_ref.refs_3_), channel_id=1, source_target_pairs={{0,2},{1,3},{2,0},{3,1},{4,6},{5,7},{6,4},{7,5},{8,10},{9,11},{10,... | collective-permute-start | bytes 417800 | tf_op jit(solution)/shard_map/ppermute | solution.py:25
  12.3 12.1 %collective-permute-start.7 = (bf16[32,2176]{1,0:T(8,128)(2,1)S(1)}, bf16[32,2176]{1,0:T(8,128)(2,1)S(1)}, u32[]{:S(2)}, u32[]{:S(2)}) collective-permute-start(bf16[32,2176]{1,0:T(8,128)(2,1)S(1)} %constant_dynamic-update-slice_fusion.after_ref.refs_3_), channel_id=1, source_target_pairs={{0,4},{1,5},{2,6},{3,7},{4,0},{5,1},{6,2},{7,3},{8,12},{9,13},{10,... | collective-permute-start | bytes 417800 | tf_op jit(solution)/shard_map/ppermute | solution.py:25
  13.1 22.8 %collective-permute-start.4 = (bf16[32,2176]{1,0:T(8,128)(2,1)S(1)}, bf16[32,2176]{1,0:T(8,128)(2,1)S(1)}, u32[]{:S(2)}, u32[]{:S(2)}) collective-permute-start(bf16[32,2176]{1,0:T(8,128)(2,1)S(1)} %constant_dynamic-update-slice_fusion.after_ref.refs_3_), channel_id=1, source_target_pairs={{0,1},{1,0},{2,3},{3,2},{4,5},{5,4},{6,7},{7,6},{8,9},{9,8},{10,11... | collective-permute-start | bytes 417800 | tf_op jit(solution)/shard_map/ppermute | solution.py:25
  17.1 18.9 %collective-permute-start.9 = (bf16[32,2176]{1,0:T(8,128)(2,1)S(1)}, bf16[32,2176]{1,0:T(8,128)(2,1)S(1)}, u32[]{:S(2)}, u32[]{:S(2)}) collective-permute-start(bf16[32,2176]{1,0:T(8,128)(2,1)S(1)} %collective-permute-done.3.after_ref.refs_9_), channel_id=1, source_target_pairs={{0,1},{1,0},{2,3},{3,2},{4,5},{5,4},{6,7},{7,6},{8,9},{9,8},{10,11... | collective-permute-start | bytes 417800 | tf_op jit(solution)/shard_map/ppermute | solution.py:25
  20.3 15.6 %collective-permute-start.6 = (bf16[32,2176]{1,0:T(8,128)(2,1)S(1)}, bf16[32,2176]{1,0:T(8,128)(2,1)S(1)}, u32[]{:S(2)}, u32[]{:S(2)}) collective-permute-start(bf16[32,2176]{1,0:T(8,128)(2,1)S(1)} %collective-permute-done.5.refs_5_), channel_id=1, source_target_pairs={{0,1},{1,0},{2,3},{3,2},{4,5},{5,4},{6,7},{7,6},{8,9},{9,8},{10,11... | collective-permute-start | bytes 417800 | tf_op jit(solution)/shard_map/ppermute | solution.py:25
  24.4 11.6 %collective-permute-start.8 = (bf16[32,2176]{1,0:T(8,128)(2,1)S(1)}, bf16[32,2176]{1,0:T(8,128)(2,1)S(1)}, u32[]{:S(2)}, u32[]{:S(2)}) collective-permute-start(bf16[32,2176]{1,0:T(8,128)(2,1)S(1)} %collective-permute-done.7.refs_7_), channel_id=1, source_target_pairs={{0,1},{1,0},{2,3},{3,2},{4,5},{5,4},{6,7},{7,6},{8,9},{9,8},{10,11... | collective-permute-start | bytes 417800 | tf_op jit(solution)/shard_map/ppermute | solution.py:25
  30.9 5.1 %copy-start.2 = (s32[1,128]{1,0:T(1,128)S(1)}, s32[1,128]{1,0:T(1,128)}, u32[]{:S(2)}) copy-start(s32[1,128]{1,0:T(1,128)} %seed_ref.1) | copy-start | bytes 1540
  35.9 31.4 %copy-start.1 = (f32[1,2048]{1,0:T(1,128)S(1)}, f32[1,2048]{1,0:T(1,128)}, u32[]{:S(2)}) copy-start(f32[1,2048]{1,0:T(1,128)} %dec_ref.3) | copy-start | bytes 24580
  35.9 41.7 %copy-start = (f32[1,4096]{1,0:T(1,128)S(1)}, f32[1,4096]{1,0:T(1,128)}, u32[]{:S(2)}) copy-start(f32[1,4096]{1,0:T(1,128)} %enc_ref.1) | copy-start | bytes 49156
  35.9 41.7 %copy-start.3 = (s32[1,128]{1,0:T(1,128)S(1)}, s32[1,128]{1,0:T(1,128)}, u32[]{:S(2)}) copy-start(s32[1,128]{1,0:T(1,128)} %dead_ref.1) | copy-start | bytes 1540
  48.9 6.4 %collective-permute-start.15 = (bf16[32,2048]{1,0:T(8,128)(2,1)S(1)}, bf16[32,2048]{1,0:T(8,128)(2,1)S(1)}, u32[]{:S(2)}, u32[]{:S(2)}) collective-permute-start(bf16[32,2048]{1,0:T(8,128)(2,1)S(1)} %get-tuple-element.62), channel_id=1, source_target_pairs={{0,1},{1,0},{2,3},{3,2},{4,5},{5,4},{6,7},{7,6},{8,9},{9,8},{10,11... | collective-permute-start | bytes 393224 | tf_op jit(solution)/shard_map/ppermute | solution.py:25
  49.4 8.6 %collective-permute-start.13 = (bf16[32,2048]{1,0:T(8,128)(2,1)S(1)}, bf16[32,2048]{1,0:T(8,128)(2,1)S(1)}, u32[]{:S(2)}, u32[]{:S(2)}) collective-permute-start(bf16[32,2048]{1,0:T(8,128)(2,1)S(1)} %get-tuple-element.60), channel_id=1, source_target_pairs={{0,1},{1,0},{2,3},{3,2},{4,5},{5,4},{6,7},{7,6},{8,9},{9,8},{10,11... | collective-permute-start | bytes 393224 | tf_op jit(solution)/shard_map/ppermute | solution.py:25
  50.9 10.0 %collective-permute-start.11 = (bf16[32,2048]{1,0:T(8,128)(2,1)S(1)}, bf16[32,2048]{1,0:T(8,128)(2,1)S(1)}, u32[]{:S(2)}, u32[]{:S(2)}) collective-permute-start(bf16[32,2048]{1,0:T(8,128)(2,1)S(1)} %get-tuple-element.58), channel_id=1, source_target_pairs={{0,1},{1,0},{2,3},{3,2},{4,5},{5,4},{6,7},{7,6},{8,9},{9,8},{10,11... | collective-permute-start | bytes 393224 | tf_op jit(solution)/shard_map/ppermute | solution.py:25
  51.4 12.2 %collective-permute-start.10 = (bf16[32,2048]{1,0:T(8,128)(2,1)S(1)}, bf16[32,2048]{1,0:T(8,128)(2,1)S(1)}, u32[]{:S(2)}, u32[]{:S(2)}) collective-permute-start(bf16[32,2048]{1,0:T(8,128)(2,1)S(1)} %get-tuple-element.56), channel_id=1, source_target_pairs={{0,1},{1,0},{2,3},{3,2},{4,5},{5,4},{6,7},{7,6},{8,9},{9,8},{10,11... | collective-permute-start | bytes 393224 | tf_op jit(solution)/shard_map/ppermute | solution.py:25
  52.9 15.4 %collective-permute-start.20 = (bf16[64,2048]{1,0:T(8,128)(2,1)S(1)}, bf16[64,2048]{1,0:T(8,128)(2,1)S(1)}, u32[]{:S(2)}, u32[]{:S(2)}) collective-permute-start(bf16[64,2048]{1,0:T(8,128)(2,1)S(1)} %get-tuple-element.70), channel_id=1, source_target_pairs={{0,1},{1,0},{2,3},{3,2},{4,5},{5,4},{6,7},{7,6},{8,9},{9,8},{10,11... | collective-permute-start | bytes 786440 | tf_op jit(solution)/shard_map/ppermute | solution.py:25
  55.3 8.4 %collective-permute-start.16 = (bf16[32,2048]{1,0:T(8,128)(2,1)S(1)}, bf16[32,2048]{1,0:T(8,128)(2,1)S(1)}, u32[]{:S(2)}, u32[]{:S(2)}) collective-permute-start(bf16[32,2048]{1,0:T(8,128)(2,1)S(1)} %add_convert_fusion), channel_id=1, source_target_pairs={{0,6},{1,7},{2,4},{3,5},{4,2},{5,3},{6,0},{7,1},{8,14},{9,15},{10,... | collective-permute-start | bytes 393224 | tf_op jit(solution)/shard_map/ppermute | solution.py:25
  58.1 8.1 %collective-permute-start.14 = (bf16[32,2048]{1,0:T(8,128)(2,1)S(1)}, bf16[32,2048]{1,0:T(8,128)(2,1)S(1)}, u32[]{:S(2)}, u32[]{:S(2)}) collective-permute-start(bf16[32,2048]{1,0:T(8,128)(2,1)S(1)} %add_convert_fusion.1), channel_id=1, source_target_pairs={{0,4},{1,5},{2,6},{3,7},{4,0},{5,1},{6,2},{7,3},{8,12},{9,13},{10,... | collective-permute-start | bytes 393224 | tf_op jit(solution)/shard_map/ppermute | solution.py:25
  60.9 6.3 %collective-permute-start.12 = (bf16[32,2048]{1,0:T(8,128)(2,1)S(1)}, bf16[32,2048]{1,0:T(8,128)(2,1)S(1)}, u32[]{:S(2)}, u32[]{:S(2)}) collective-permute-start(bf16[32,2048]{1,0:T(8,128)(2,1)S(1)} %add_convert_fusion.2), channel_id=1, source_target_pairs={{0,2},{1,3},{2,0},{3,1},{4,6},{5,7},{6,4},{7,5},{8,10},{9,11},{10,... | collective-permute-start | bytes 393224 | tf_op jit(solution)/shard_map/ppermute | solution.py:25
  67.5 3.7 %collective-permute-start.21 = (f32[8,128]{1,0:T(8,128)S(1)}, f32[8,128]{1,0:T(8,128)S(1)}, u32[]{:S(2)}, u32[]{:S(2)}) collective-permute-start(f32[8,128]{1,0:T(8,128)S(1)} %get-tuple-element.71.refs_2_), channel_id=1, source_target_pairs={{0,1},{1,0},{2,3},{3,2},{4,5},{5,4},{6,7},{7,6},{8,9},{9,8},{10,11... | collective-permute-start | bytes 12296 | tf_op jit(solution)/shard_map/ppermute | solution.py:25
  71.3 10.2 %collective-permute-start.22 = (bf16[16,2176]{1,0:T(8,128)(2,1)S(1)}, bf16[16,2176]{1,0:T(8,128)(2,1)S(1)}, u32[]{:S(2)}, u32[]{:S(2)}) collective-permute-start(bf16[16,2176]{1,0:T(8,128)(2,1)S(1)} %get-tuple-element.74), channel_id=1, source_target_pairs={{0,2},{1,3},{2,0},{3,1},{4,6},{5,7},{6,4},{7,5},{8,10},{9,11},{10,... | collective-permute-start | bytes 208904 | tf_op jit(solution)/shard_map/ppermute | solution.py:25
  71.4 10.1 %collective-permute-start.23 = (bf16[16,2176]{1,0:T(8,128)(2,1)S(1)}, bf16[16,2176]{1,0:T(8,128)(2,1)S(1)}, u32[]{:S(2)}, u32[]{:S(2)}) collective-permute-start(bf16[16,2176]{1,0:T(8,128)(2,1)S(1)} %get-tuple-element.75), channel_id=1, source_target_pairs={{0,4},{1,5},{2,6},{3,7},{4,0},{5,1},{6,2},{7,3},{8,12},{9,13},{10,... | collective-permute-start | bytes 208904 | tf_op jit(solution)/shard_map/ppermute | solution.py:25
  74.5 7.0 %collective-permute-start.24 = (bf16[16,2176]{1,0:T(8,128)(2,1)S(1)}, bf16[16,2176]{1,0:T(8,128)(2,1)S(1)}, u32[]{:S(2)}, u32[]{:S(2)}) collective-permute-start(bf16[16,2176]{1,0:T(8,128)(2,1)S(1)} %get-tuple-element.76), channel_id=1, source_target_pairs={{0,6},{1,7},{2,4},{3,5},{4,2},{5,3},{6,0},{7,1},{8,14},{9,15},{10,... | collective-permute-start | bytes 208904 | tf_op jit(solution)/shard_map/ppermute | solution.py:25
  75.7 1.2 %collective-permute-start.17 = (bf16[8,2048]{1,0:T(8,128)(2,1)S(1)}, bf16[8,2048]{1,0:T(8,128)(2,1)S(1)}, u32[]{:S(2)}, u32[]{:S(2)}) collective-permute-start(bf16[8,2048]{1,0:T(8,128)(2,1)S(1)} %get-tuple-element.64), channel_id=1, source_target_pairs={{0,8},{8,0},{16,24},{24,16},{1,9},{9,1},{17,25},{25,17},{2,10},{10... | collective-permute-start | bytes 98312 | tf_op jit(solution)/shard_map/ppermute | solution.py:25
  75.7 3.9 %collective-permute-start.18 = (bf16[8,2048]{1,0:T(8,128)(2,1)S(1)}, bf16[8,2048]{1,0:T(8,128)(2,1)S(1)}, u32[]{:S(2)}, u32[]{:S(2)}) collective-permute-start(bf16[8,2048]{1,0:T(8,128)(2,1)S(1)} %get-tuple-element.65), channel_id=1, source_target_pairs={{0,16},{8,24},{16,0},{24,8},{1,17},{9,25},{17,1},{25,9},{2,18},{10... | collective-permute-start | bytes 98312 | tf_op jit(solution)/shard_map/ppermute | solution.py:25
  76.9 3.3 %collective-permute-start.19 = (bf16[8,2048]{1,0:T(8,128)(2,1)S(1)}, bf16[8,2048]{1,0:T(8,128)(2,1)S(1)}, u32[]{:S(2)}, u32[]{:S(2)}) collective-permute-start(bf16[8,2048]{1,0:T(8,128)(2,1)S(1)} %get-tuple-element.66), channel_id=1, source_target_pairs={{0,24},{8,16},{16,8},{24,0},{1,25},{9,17},{17,9},{25,1},{2,26},{10... | collective-permute-start | bytes 98312 | tf_op jit(solution)/shard_map/ppermute | solution.py:25
